TPU v7x, 32 devices: a whole 2x2x4 slice. The times are simulated.
32 devices in a mesh: gx: 4 (over z), gy: 4 (over y, core), gz: 2 (over x).
Axes of the slice: x: 2, y: 2, z: 4, core: 2. Of those that a mesh axis runs over, the one named last changes fastest.
Arguments:
- source: float32 [32, 64, 512], P('gx', 'gy', 'gz'), may hold values from -4 to 4
- conduct: float32 [32, 64, 512], P('gx', 'gy', 'gz'), may hold values from 0.5 to 2
- solid_mask: int32 [32, 64, 512], P('gx', 'gy', 'gz'), may hold values 0 or 1
- line_ids: int32 [4, 4, 2, 16], P('gx', 'gy'), may hold values from -1 to 31, as said below
Outputs:
- pressure: float32 [32, 64, 512], P('gx', 'gy', 'gz')
Inputs may be any that keep to these rules, and one draw needn't show every extreme that they name: Entries of line_ids[g, h, o, :] are numbers a * 8 + b of coarse columns (coarse cells [a, b, :] of every device with gx index g and gy index h), padded at the end with -1; no column is listed twice for one (g, h); every owner o lists at least one, and for every (g, h) some owner fills all 16 slots.
All inputs are finite; a program needn't handle non-finite values. No bound on the sum of `solid_mask` on one device may be relied on, other than what follows from the above.
Results may differ from a plain program's by a relative error of at most 0.00055.
Values sent between devices are 32-bit elements; how exact they have to be, the bound alone decides.
A program may use at most 64 MiB of HBM per device.

v0:
```python
import jax
import jax.numpy as jnp
from jax import lax
from jax.sharding import PartitionSpec as P

CZ = 256
SWEEPS = 2


clog_factor = 0.2
shift_fine = 0.001


def padded_2(cells, sides, width):
    for axis, dim in sides:
        count = lax.axis_size(axis)
        ends = count - 1
        head = lax.slice_in_dim(cells, 0, width, axis=dim)
        tail = lax.slice_in_dim(cells, cells.shape[dim] - width, cells.shape[dim], axis=dim)
        cells = jnp.concatenate(
            [
                lax.ppermute(tail, axis, [(i, (i + 1) % count) for i in range(ends)]),
                cells,
                lax.ppermute(head, axis, [((i + 1) % count, i) for i in range(ends)]),
            ],
            axis=dim,
        )
    return cells


def neighbours(padded):
    return [
        padded[2:, 1:-1, 1:-1],
        padded[:-2, 1:-1, 1:-1],
        padded[1:-1, 2:, 1:-1],
        padded[1:-1, :-2, 1:-1],
        padded[1:-1, 1:-1, 2:],
        padded[1:-1, 1:-1, :-2],
    ]


def face_weights(padded_cond):
    centre = padded_cond[1:-1, 1:-1, 1:-1]
    weights = [0.5 * (centre + beside) for beside in neighbours(padded_cond)]
    diagonal = (
        shift_fine + weights[0] + weights[1] + weights[2] + weights[3] + weights[4] + weights[5]
    )
    return (weights, diagonal)


def inflow_of(padded, weights):
    besides = neighbours(padded)
    inflow = weights[0] * besides[0]
    for weight, beside in zip(weights[1:], besides[1:]):
        inflow = inflow + weight * beside
    return inflow


def parity_of(extent):
    along_x = jnp.arange(extent[0], dtype=jnp.int32)[:, None, None]
    along_y = jnp.arange(extent[1], dtype=jnp.int32)[None, :, None]
    along_z = jnp.arange(extent[2], dtype=jnp.int32)[None, None, :]
    return (along_x + along_y + along_z) % 2


def block_mean(values):
    extent = values.shape
    return values.reshape(extent[0] // 2, 2, extent[1] // 2, 2, extent[2] // 2, 2).mean(
        axis=(1, 3, 5)
    )


def prolong(coarse):
    return jnp.repeat(jnp.repeat(jnp.repeat(coarse, 2, axis=0), 2, axis=1), 2, axis=2)


def from_earlier(values, stride, fill):
    edge = jnp.full(values[..., :stride].shape, fill, values.dtype)
    return jnp.concatenate([edge, values[..., :-stride]], axis=-1)


def from_later(values, stride, fill):
    edge = jnp.full(values[..., -stride:].shape, fill, values.dtype)
    return jnp.concatenate([values[..., stride:], edge], axis=-1)


def line_solve(line_rhs, line_cond):
    screen = 1.0 / (CZ * CZ)
    pair_sums = line_cond[..., :-1] + line_cond[..., 1:]
    left_sum = jnp.concatenate([line_cond[..., :1], pair_sums], axis=-1)
    right_sum = jnp.concatenate([pair_sums, line_cond[..., -1:]], axis=-1)
    main_diag = screen + left_sum + right_sum
    zero_col = jnp.zeros_like(line_cond[..., :1])
    lower_diag = jnp.concatenate([zero_col, -pair_sums], axis=-1)
    upper_diag = jnp.concatenate([-pair_sums, zero_col], axis=-1)
    values = line_rhs
    length = line_rhs.shape[-1]
    stride = 1
    while stride < length:
        lower_prev = from_earlier(lower_diag, stride, 0.0)
        main_prev = from_earlier(main_diag, stride, 1.0)
        upper_prev = from_earlier(upper_diag, stride, 0.0)
        value_prev = from_earlier(values, stride, 0.0)
        lower_next = from_later(lower_diag, stride, 0.0)
        main_next = from_later(main_diag, stride, 1.0)
        upper_next = from_later(upper_diag, stride, 0.0)
        value_next = from_later(values, stride, 0.0)
        factor_low = -lower_diag / main_prev
        factor_high = -upper_diag / main_next
        main_diag = main_diag + factor_low * upper_prev + factor_high * lower_next
        values = values + factor_low * value_prev + factor_high * value_next
        lower_diag = factor_low * lower_prev
        upper_diag = factor_high * upper_next
        stride = stride * 2
    return values / main_diag


def face_halo(values):
    return padded_2(values, (("gx", 0), ("gy", 1), ("gz", 2)), 1)


def solve_rows(pieces):
    rhs_parts, cond_parts = pieces
    owners, slot_count, length = rhs_parts.shape
    line_rhs = jnp.transpose(rhs_parts, (1, 0, 2)).reshape(slot_count, owners * length)
    line_cond = jnp.transpose(cond_parts, (1, 0, 2)).reshape(slot_count, owners * length)
    solved = line_solve(line_rhs, line_cond)
    back_rows = jnp.transpose(solved.reshape(slot_count, owners, length), (1, 0, 2))
    return lax.all_to_all(back_rows, "gz", split_axis=0, concat_axis=0, tiled=True)


def shards(source, conduct, solid_mask, line_ids):
    relax_weight = 2.0 / (CZ * CZ)
    clogged = conduct * jnp.where(solid_mask > 0, clog_factor, 1.0)
    colours = parity_of(source.shape)
    padded_cond = padded_2(clogged, (("gx", 0), ("gy", 1), ("gz", 2)), 1)
    weights, diagonal = face_weights(padded_cond)

    def smoother(pressure):
        for colour in (0, 1):
            updated = (source + inflow_of(face_halo(pressure), weights)) / diagonal
            pressure = jnp.where(colours == colour, updated, pressure)
        return pressure

    pressure = jnp.zeros_like(source)
    for sweep_no in range(SWEEPS):
        pressure = smoother(pressure)
    residual = source - (diagonal * pressure - inflow_of(face_halo(pressure), weights))
    coarse_rhs = block_mean(residual)
    coarse_extent = coarse_rhs.shape
    coarse_rhs = coarse_rhs.reshape(-1, coarse_extent[2])
    coarse_cond = block_mean(clogged).reshape(-1, coarse_extent[2])
    slot_ids = line_ids.reshape(-1)
    selector = (
        slot_ids[:, None] == jnp.arange(coarse_rhs.shape[0], dtype=jnp.int32)[None, :]
    ).astype(jnp.float32)
    send_rhs = jnp.dot(selector, coarse_rhs, precision=lax.Precision.HIGHEST)
    send_cond = jnp.dot(selector, coarse_cond, precision=lax.Precision.HIGHEST)
    send_rhs = send_rhs.reshape(line_ids.shape[2], line_ids.shape[3], coarse_extent[2])
    send_cond = send_cond.reshape(line_ids.shape[2], line_ids.shape[3], coarse_extent[2])
    returned = solve_rows(
        (
            lax.all_to_all(send_rhs, "gz", split_axis=0, concat_axis=0, tiled=True),
            lax.all_to_all(send_cond, "gz", split_axis=0, concat_axis=0, tiled=True),
        )
    )
    correction = jnp.dot(
        selector.T, returned.reshape(-1, coarse_extent[2]), precision=lax.Precision.HIGHEST
    )
    correction = correction.reshape(coarse_extent)
    pressure = pressure + relax_weight * prolong(correction)
    for sweep_no in range(SWEEPS):
        pressure = smoother(pressure)
    return pressure


def solution(mesh):
    in_specs = (
        P("gx", "gy", "gz"),
        P("gx", "gy", "gz"),
        P("gx", "gy", "gz"),
        P("gx", "gy", None, None),
    )
    out_specs = P("gx", "gy", "gz")
    return jax.shard_map(shards, mesh=mesh, in_specs=in_specs, out_specs=out_specs, check_vma=False)
```

profile of v0, /device:TPU:1, one launch (start us, length us, event | category | flops | bytes accessed | tf_op | source)
XLA Modules:
  0.0 274.0 jit_solution(3257809136630898557)
XLA Ops:
  2.3 4.7 %collective-permute-start.2 = (f32[1,16,256]{2,1,0:T(8,128)S(1)}, f32[1,16,256]{2,1,0:T(8,128)S(1)}, u32[]{:S(2)}, u32[]{:S(2)}) collective-permute-start(f32[1,16,256]{2,1,0:T(8,128)S(1)} %get-tuple-element.86), channel_id=1, source_target_pairs={{0,8},{8,16},{16,24},{1,9},{9,17},{17,25},{2,10},{10,18},{18,26},{... | collective-permute-start | bytes 49160 | tf_op jit(solution)/shard_map/ppermute | solution.py:22
  36.6 4.2 %collective-permute-done.9 = f32[10,18,1]{2,1,0:T(8,128)S(1)} collective-permute-done((f32[10,18,1]{2,1,0:T(8,128)S(1)}, f32[10,18,1]{2,1,0:T(8,128)S(1)}, u32[]{:S(2)}, u32[]{:S(2)}) %collective-permute-start.9) | collective-permute-done | bytes 752 | tf_op jit(solution)/shard_map/ppermute | solution.py:24
  65.0 4.5 %collective-permute-start.19 = (f32[1,16,256]{2,1,0:T(8,128)S(1)}, f32[1,16,256]{2,1,0:T(8,128)S(1)}, u32[]{:S(2)}, u32[]{:S(2)}) collective-permute-start(f32[1,16,256]{2,1,0:T(8,128)S(1)} %get-tuple-element.82), channel_id=1, source_target_pairs={{0,8},{8,16},{16,24},{1,9},{9,17},{17,25},{2,10},{10,18},{18,26},{... | collective-permute-start | bytes 49160 | tf_op jit(solution)/shard_map/ppermute | solution.py:22
  70.4 4.0 %collective-permute-start.20 = (f32[10,1,256]{2,1,0:T(1,128)S(1)}, f32[10,1,256]{2,1,0:T(1,128)S(1)}, u32[]{:S(2)}, u32[]{:S(2)}) collective-permute-start(f32[10,1,256]{2,1,0:T(1,128)S(1)} %get-tuple-element.63), channel_id=1, source_target_pairs={{2,0},{4,2},{6,4},{3,1},{5,3},{7,5},{10,8},{12,10},{14,12},{11,9},... | collective-permute-start | bytes 30728 | tf_op jit(solution)/shard_map/ppermute | solution.py:24
  80.1 4.2 %collective-permute-start.23 = (f32[10,18,1]{2,1,0:T(8,128)S(1)}, f32[10,18,1]{2,1,0:T(8,128)S(1)}, u32[]{:S(2)}, u32[]{:S(2)}) collective-permute-start(f32[10,18,1]{2,1,0:T(8,128)S(1)} %get-tuple-element.43), channel_id=1, source_target_pairs={{0,1},{2,3},{4,5},{6,7},{8,9},{10,11},{12,13},{14,15},{16,17},{18,... | collective-permute-start | bytes 2168 | tf_op jit(solution)/shard_map/ppermute | solution.py:22
  84.3 9.8 %reshape.121 = f32[4,2,8,2,128,2]{5,4,3,2,1,0:T(8,128)} reshape(f32[8,16,256]{2,1,0:T(8,128)S(1)} %select_multiply_fusion) | data formatting | bytes 262144 | tf_op jit(solution)/shard_map/reshape | solution.py:68
  94.1 4.0 %reduce_sum.19 = f32[4,8,128]{2,1,0:T(8,128)S(1)} reduce(f32[4,2,8,2,128,2]{5,4,3,2,1,0:T(8,128)} %reshape.121, f32[]{:T(128)} %constant.18.clone.1), dimensions={1,3,5}, to_apply=%region_1.2 | reduce | flops 28672 | bytes 147460 | tf_op jit(solution)/shard_map/reduce_sum | solution.py:68
  99.7 4.5 %collective-permute-start.25 = (f32[1,16,256]{2,1,0:T(8,128)S(1)}, f32[1,16,256]{2,1,0:T(8,128)S(1)}, u32[]{:S(2)}, u32[]{:S(2)}) collective-permute-start(f32[1,16,256]{2,1,0:T(8,128)S(1)} %get-tuple-element.80), channel_id=1, source_target_pairs={{0,8},{8,16},{16,24},{1,9},{9,17},{17,25},{2,10},{10,18},{18,26},{... | collective-permute-start | bytes 49160 | tf_op jit(solution)/shard_map/ppermute | solution.py:22
  110.3 5.0 %collective-permute-start.27 = (f32[10,1,256]{2,1,0:T(1,128)S(1)}, f32[10,1,256]{2,1,0:T(1,128)S(1)}, u32[]{:S(2)}, u32[]{:S(2)}) collective-permute-start(f32[10,1,256]{2,1,0:T(1,128)S(1)} %get-tuple-element.60), channel_id=1, source_target_pairs={{0,2},{2,4},{4,6},{1,3},{3,5},{5,7},{8,10},{10,12},{12,14},{9,11},... | collective-permute-start | bytes 30728 | tf_op jit(solution)/shard_map/ppermute | solution.py:22
  124.9 4.3 %collective-permute-start.31 = (f32[1,16,256]{2,1,0:T(8,128)S(1)}, f32[1,16,256]{2,1,0:T(8,128)S(1)}, u32[]{:S(2)}, u32[]{:S(2)}) collective-permute-start(f32[1,16,256]{2,1,0:T(8,128)S(1)} %get-tuple-element.78), channel_id=1, source_target_pairs={{0,8},{8,16},{16,24},{1,9},{9,17},{17,25},{2,10},{10,18},{18,26},{... | collective-permute-start | bytes 49160 | tf_op jit(solution)/shard_map/ppermute | solution.py:22
  132.0 6.2 %collective-permute-start.33 = (f32[10,1,256]{2,1,0:T(1,128)S(1)}, f32[10,1,256]{2,1,0:T(1,128)S(1)}, u32[]{:S(2)}, u32[]{:S(2)}) collective-permute-start(f32[10,1,256]{2,1,0:T(1,128)S(1)} %get-tuple-element.58), channel_id=1, source_target_pairs={{0,2},{2,4},{4,6},{1,3},{3,5},{5,7},{8,10},{10,12},{12,14},{9,11},... | collective-permute-start | bytes 30728 | tf_op jit(solution)/shard_map/ppermute | solution.py:22
  140.4 4.1 %collective-permute-start.35 = (f32[10,18,1]{2,1,0:T(8,128)S(1)}, f32[10,18,1]{2,1,0:T(8,128)S(1)}, u32[]{:S(2)}, u32[]{:S(2)}) collective-permute-start(f32[10,18,1]{2,1,0:T(8,128)S(1)} %get-tuple-element.39), channel_id=1, source_target_pairs={{0,1},{2,3},{4,5},{6,7},{8,9},{10,11},{12,13},{14,15},{16,17},{18,... | collective-permute-start | bytes 2168 | tf_op jit(solution)/shard_map/ppermute | solution.py:22
  146.6 9.8 %reshape.119 = f32[4,2,8,2,128,2]{5,4,3,2,1,0:T(8,128)} reshape(f32[8,16,256]{2,1,0:T(8,128)S(1)} %fusion.69) | data formatting | bytes 262144 | tf_op jit(solution)/shard_map/reshape | solution.py:68
  179.4 4.5 %collective-permute-start.37 = (f32[1,16,256]{2,1,0:T(8,128)S(1)}, f32[1,16,256]{2,1,0:T(8,128)S(1)}, u32[]{:S(2)}, u32[]{:S(2)}) collective-permute-start(f32[1,16,256]{2,1,0:T(8,128)S(1)} %get-tuple-element.76), channel_id=1, source_target_pairs={{0,8},{8,16},{16,24},{1,9},{9,17},{17,25},{2,10},{10,18},{18,26},{... | collective-permute-start | bytes 49160 | tf_op jit(solution)/shard_map/ppermute | solution.py:22
  187.0 8.2 %collective-permute-start.39 = (f32[10,1,256]{2,1,0:T(1,128)S(1)}, f32[10,1,256]{2,1,0:T(1,128)S(1)}, u32[]{:S(2)}, u32[]{:S(2)}) collective-permute-start(f32[10,1,256]{2,1,0:T(1,128)S(1)} %get-tuple-element.56), channel_id=1, source_target_pairs={{0,2},{2,4},{4,6},{1,3},{3,5},{5,7},{8,10},{10,12},{12,14},{9,11},... | collective-permute-start | bytes 30728 | tf_op jit(solution)/shard_map/ppermute | solution.py:22
  204.9 4.5 %collective-permute-start.43 = (f32[1,16,256]{2,1,0:T(8,128)S(1)}, f32[1,16,256]{2,1,0:T(8,128)S(1)}, u32[]{:S(2)}, u32[]{:S(2)}) collective-permute-start(f32[1,16,256]{2,1,0:T(8,128)S(1)} %get-tuple-element.74), channel_id=1, source_target_pairs={{0,8},{8,16},{16,24},{1,9},{9,17},{17,25},{2,10},{10,18},{18,26},{... | collective-permute-start | bytes 49160 | tf_op jit(solution)/shard_map/ppermute | solution.py:22
  212.3 6.2 %collective-permute-start.45 = (f32[10,1,256]{2,1,0:T(1,128)S(1)}, f32[10,1,256]{2,1,0:T(1,128)S(1)}, u32[]{:S(2)}, u32[]{:S(2)}) collective-permute-start(f32[10,1,256]{2,1,0:T(1,128)S(1)} %get-tuple-element.54), channel_id=1, source_target_pairs={{0,2},{2,4},{4,6},{1,3},{3,5},{5,7},{8,10},{10,12},{12,14},{9,11},... | collective-permute-start | bytes 30728 | tf_op jit(solution)/shard_map/ppermute | solution.py:22
  220.7 4.1 %collective-permute-start.47 = (f32[10,18,1]{2,1,0:T(8,128)S(1)}, f32[10,18,1]{2,1,0:T(8,128)S(1)}, u32[]{:S(2)}, u32[]{:S(2)}) collective-permute-start(f32[10,18,1]{2,1,0:T(8,128)S(1)} %get-tuple-element.35), channel_id=1, source_target_pairs={{0,1},{2,3},{4,5},{6,7},{8,9},{10,11},{12,13},{14,15},{16,17},{18,... | collective-permute-start | bytes 2168 | tf_op jit(solution)/shard_map/ppermute | solution.py:22
  228.2 4.5 %collective-permute-start.49 = (f32[1,16,256]{2,1,0:T(8,128)S(1)}, f32[1,16,256]{2,1,0:T(8,128)S(1)}, u32[]{:S(2)}, u32[]{:S(2)}) collective-permute-start(f32[1,16,256]{2,1,0:T(8,128)S(1)} %get-tuple-element.72), channel_id=1, source_target_pairs={{0,8},{8,16},{16,24},{1,9},{9,17},{17,25},{2,10},{10,18},{18,26},{... | collective-permute-start | bytes 49160 | tf_op jit(solution)/shard_map/ppermute | solution.py:22
  235.6 6.1 %collective-permute-start.51 = (f32[10,1,256]{2,1,0:T(1,128)S(1)}, f32[10,1,256]{2,1,0:T(1,128)S(1)}, u32[]{:S(2)}, u32[]{:S(2)}) collective-permute-start(f32[10,1,256]{2,1,0:T(1,128)S(1)} %get-tuple-element.52), channel_id=1, source_target_pairs={{0,2},{2,4},{4,6},{1,3},{3,5},{5,7},{8,10},{10,12},{12,14},{9,11},... | collective-permute-start | bytes 30728 | tf_op jit(solution)/shard_map/ppermute | solution.py:22
  243.9 4.1 %collective-permute-start.53 = (f32[10,18,1]{2,1,0:T(8,128)S(1)}, f32[10,18,1]{2,1,0:T(8,128)S(1)}, u32[]{:S(2)}, u32[]{:S(2)}) collective-permute-start(f32[10,18,1]{2,1,0:T(8,128)S(1)} %get-tuple-element.33), channel_id=1, source_target_pairs={{0,1},{2,3},{4,5},{6,7},{8,9},{10,11},{12,13},{14,15},{16,17},{18,... | collective-permute-start | bytes 2168 | tf_op jit(solution)/shard_map/ppermute | solution.py:22
  251.4 4.5 %collective-permute-start.55 = (f32[1,16,256]{2,1,0:T(8,128)S(1)}, f32[1,16,256]{2,1,0:T(8,128)S(1)}, u32[]{:S(2)}, u32[]{:S(2)}) collective-permute-start(f32[1,16,256]{2,1,0:T(8,128)S(1)} %get-tuple-element.70), channel_id=1, source_target_pairs={{0,8},{8,16},{16,24},{1,9},{9,17},{17,25},{2,10},{10,18},{18,26},{... | collective-permute-start | bytes 49160 | tf_op jit(solution)/shard_map/ppermute | solution.py:22
  258.8 6.1 %collective-permute-start.57 = (f32[10,1,256]{2,1,0:T(1,128)S(1)}, f32[10,1,256]{2,1,0:T(1,128)S(1)}, u32[]{:S(2)}, u32[]{:S(2)}) collective-permute-start(f32[10,1,256]{2,1,0:T(1,128)S(1)} %get-tuple-element.50), channel_id=1, source_target_pairs={{0,2},{2,4},{4,6},{1,3},{3,5},{5,7},{8,10},{10,12},{12,14},{9,11},... | collective-permute-start | bytes 30728 | tf_op jit(solution)/shard_map/ppermute | solution.py:22
  267.1 4.1 %collective-permute-start.59 = (f32[10,18,1]{2,1,0:T(8,128)S(1)}, f32[10,18,1]{2,1,0:T(8,128)S(1)}, u32[]{:S(2)}, u32[]{:S(2)}) collective-permute-start(f32[10,18,1]{2,1,0:T(8,128)S(1)} %get-tuple-element.31), channel_id=1, source_target_pairs={{0,1},{2,3},{4,5},{6,7},{8,9},{10,11},{12,13},{14,15},{16,17},{18,... | collective-permute-start | bytes 2168 | tf_op jit(solution)/shard_map/ppermute | solution.py:22
  (225 shorter events, 146.4 us)
Async XLA Ops:
  1.0 11.3 %collective-permute-start = (f32[1,16,256]{2,1,0:T(8,128)S(1)}, f32[1,16,256]{2,1,0:T(8,128)S(1)}, u32[]{:S(2)}, u32[]{:S(2)}) collective-permute-start(f32[1,16,256]{2,1,0:T(8,128)S(1)} %get-tuple-element.87), channel_id=1, source_target_pairs={{8,0},{16,8},{24,16},{9,1},{17,9},{25,17},{10,2},{18,10},{26,18},{... | collective-permute-start | bytes 49160 | tf_op jit(solution)/shard_map/ppermute | solution.py:24
  2.3 10.0 %collective-permute-start.2 = (f32[1,16,256]{2,1,0:T(8,128)S(1)}, f32[1,16,256]{2,1,0:T(8,128)S(1)}, u32[]{:S(2)}, u32[]{:S(2)}) collective-permute-start(f32[1,16,256]{2,1,0:T(8,128)S(1)} %get-tuple-element.86), channel_id=1, source_target_pairs={{0,8},{8,16},{16,24},{1,9},{9,17},{17,25},{2,10},{10,18},{18,26},{... | collective-permute-start | bytes 49160 | tf_op jit(solution)/shard_map/ppermute | solution.py:22
  7.0 12.3 %collective-permute-start.1 = (f32[1,16,256]{2,1,0:T(8,128)S(1)}, f32[1,16,256]{2,1,0:T(8,128)S(1)}, u32[]{:S(2)}, u32[]{:S(2)}) collective-permute-start(f32[1,16,256]{2,1,0:T(8,128)S(1)} %broadcast.251), channel_id=1, source_target_pairs={{8,0},{16,8},{24,16},{9,1},{17,9},{25,17},{10,2},{18,10},{26,18},{... | collective-permute-start | bytes 49160 | tf_op jit(solution)/shard_map/ppermute | solution.py:24
  8.3 11.0 %collective-permute-start.3 = (f32[1,16,256]{2,1,0:T(8,128)S(1)}, f32[1,16,256]{2,1,0:T(8,128)S(1)}, u32[]{:S(2)}, u32[]{:S(2)}) collective-permute-start(f32[1,16,256]{2,1,0:T(8,128)S(1)} %broadcast.251), channel_id=1, source_target_pairs={{0,8},{8,16},{16,24},{1,9},{9,17},{17,25},{2,10},{10,18},{18,26},{... | collective-permute-start | bytes 49160 | tf_op jit(solution)/shard_map/ppermute | solution.py:22
  12.3 12.6 %collective-permute-start.4 = (f32[10,1,256]{2,1,0:T(1,128)S(1)}, f32[10,1,256]{2,1,0:T(1,128)S(1)}, u32[]{:S(2)}, u32[]{:S(2)}) collective-permute-start(f32[10,1,256]{2,1,0:T(1,128)S(1)} %get-tuple-element.67), channel_id=1, source_target_pairs={{2,0},{4,2},{6,4},{3,1},{5,3},{7,5},{10,8},{12,10},{14,12},{11,9},... | collective-permute-start | bytes 30728 | tf_op jit(solution)/shard_map/ppermute | solution.py:24
  15.8 9.1 %collective-permute-start.6 = (f32[10,1,256]{2,1,0:T(1,128)S(1)}, f32[10,1,256]{2,1,0:T(1,128)S(1)}, u32[]{:S(2)}, u32[]{:S(2)}) collective-permute-start(f32[10,1,256]{2,1,0:T(1,128)S(1)} %get-tuple-element.66), channel_id=1, source_target_pairs={{0,2},{2,4},{4,6},{1,3},{3,5},{5,7},{8,10},{10,12},{12,14},{9,11},... | collective-permute-start | bytes 30728 | tf_op jit(solution)/shard_map/ppermute | solution.py:22
  19.3 10.2 %collective-permute-start.5 = (f32[10,1,256]{2,1,0:T(1,128)S(1)}, f32[10,1,256]{2,1,0:T(1,128)S(1)}, u32[]{:S(2)}, u32[]{:S(2)}) collective-permute-start(f32[10,1,256]{2,1,0:T(1,128)S(1)} %get-tuple-element.69), channel_id=1, source_target_pairs={{2,0},{4,2},{6,4},{3,1},{5,3},{7,5},{10,8},{12,10},{14,12},{11,9},... | collective-permute-start | bytes 30728 | tf_op jit(solution)/shard_map/ppermute | solution.py:24
  21.2 8.3 %collective-permute-start.7 = (f32[10,1,256]{2,1,0:T(1,128)S(1)}, f32[10,1,256]{2,1,0:T(1,128)S(1)}, u32[]{:S(2)}, u32[]{:S(2)}) collective-permute-start(f32[10,1,256]{2,1,0:T(1,128)S(1)} %get-tuple-element.68), channel_id=1, source_target_pairs={{0,2},{2,4},{4,6},{1,3},{3,5},{5,7},{8,10},{10,12},{12,14},{9,11},... | collective-permute-start | bytes 30728 | tf_op jit(solution)/shard_map/ppermute | solution.py:22
  25.1 9.9 %collective-permute-start.10 = (f32[10,18,1]{2,1,0:T(8,128)S(1)}, f32[10,18,1]{2,1,0:T(8,128)S(1)}, u32[]{:S(2)}, u32[]{:S(2)}) collective-permute-start(f32[10,18,1]{2,1,0:T(8,128)S(1)} %get-tuple-element.46), channel_id=1, source_target_pairs={{0,1},{2,3},{4,5},{6,7},{8,9},{10,11},{12,13},{14,15},{16,17},{18,... | collective-permute-start | bytes 2168 | tf_op jit(solution)/shard_map/ppermute | solution.py:22
  33.6 7.2 %collective-permute-start.9 = (f32[10,18,1]{2,1,0:T(8,128)S(1)}, f32[10,18,1]{2,1,0:T(8,128)S(1)}, u32[]{:S(2)}, u32[]{:S(2)}) collective-permute-start(f32[10,18,1]{2,1,0:T(8,128)S(1)} %get-tuple-element.48), channel_id=1, source_target_pairs={{1,0},{3,2},{5,4},{7,6},{9,8},{11,10},{13,12},{15,14},{17,16},{19,... | collective-permute-start | bytes 2168 | tf_op jit(solution)/shard_map/ppermute | solution.py:24
  70.4 7.4 %collective-permute-start.20 = (f32[10,1,256]{2,1,0:T(1,128)S(1)}, f32[10,1,256]{2,1,0:T(1,128)S(1)}, u32[]{:S(2)}, u32[]{:S(2)}) collective-permute-start(f32[10,1,256]{2,1,0:T(1,128)S(1)} %get-tuple-element.63), channel_id=1, source_target_pairs={{2,0},{4,2},{6,4},{3,1},{5,3},{7,5},{10,8},{12,10},{14,12},{11,9},... | collective-permute-start | bytes 30728 | tf_op jit(solution)/shard_map/ppermute | solution.py:24
  78.8 19.3 %collective-permute-start.22 = (f32[10,18,1]{2,1,0:T(8,128)S(1)}, f32[10,18,1]{2,1,0:T(8,128)S(1)}, u32[]{:S(2)}, u32[]{:S(2)}) collective-permute-start(f32[10,18,1]{2,1,0:T(8,128)S(1)} %get-tuple-element.42), channel_id=1, source_target_pairs={{1,0},{3,2},{5,4},{7,6},{9,8},{11,10},{13,12},{15,14},{17,16},{19,... | collective-permute-start | bytes 2168 | tf_op jit(solution)/shard_map/ppermute | solution.py:24
  80.1 18.0 %collective-permute-start.23 = (f32[10,18,1]{2,1,0:T(8,128)S(1)}, f32[10,18,1]{2,1,0:T(8,128)S(1)}, u32[]{:S(2)}, u32[]{:S(2)}) collective-permute-start(f32[10,18,1]{2,1,0:T(8,128)S(1)} %get-tuple-element.43), channel_id=1, source_target_pairs={{0,1},{2,3},{4,5},{6,7},{8,9},{10,11},{12,13},{14,15},{16,17},{18,... | collective-permute-start | bytes 2168 | tf_op jit(solution)/shard_map/ppermute | solution.py:22
  98.4 9.9 %collective-permute-start.24 = (f32[1,16,256]{2,1,0:T(8,128)S(1)}, f32[1,16,256]{2,1,0:T(8,128)S(1)}, u32[]{:S(2)}, u32[]{:S(2)}) collective-permute-start(f32[1,16,256]{2,1,0:T(8,128)S(1)} %get-tuple-element.81), channel_id=1, source_target_pairs={{8,0},{16,8},{24,16},{9,1},{17,9},{25,17},{10,2},{18,10},{26,18},{... | collective-permute-start | bytes 49160 | tf_op jit(solution)/shard_map/ppermute | solution.py:24
  99.7 8.6 %collective-permute-start.25 = (f32[1,16,256]{2,1,0:T(8,128)S(1)}, f32[1,16,256]{2,1,0:T(8,128)S(1)}, u32[]{:S(2)}, u32[]{:S(2)}) collective-permute-start(f32[1,16,256]{2,1,0:T(8,128)S(1)} %get-tuple-element.80), channel_id=1, source_target_pairs={{0,8},{8,16},{16,24},{1,9},{9,17},{17,25},{2,10},{10,18},{18,26},{... | collective-permute-start | bytes 49160 | tf_op jit(solution)/shard_map/ppermute | solution.py:22
  105.1 10.2 %all-to-all-start.1 = ((f32[2,16,128]{2,1,0:T(8,128)}), f32[2,16,128]{2,1,0:T(8,128)S(1)}, u32[]{:S(2)}, u32[]{:S(2)}) async-start(f32[2,16,128]{2,1,0:T(8,128)} %fusion.142), calls=%async_computation.1 | async-start | bytes 32768 | tf_op jit(solution)/shard_map/all_to_all | solution.py:164
  130.1 8.2 %collective-permute-start.32 = (f32[10,1,256]{2,1,0:T(1,128)S(1)}, f32[10,1,256]{2,1,0:T(1,128)S(1)}, u32[]{:S(2)}, u32[]{:S(2)}) collective-permute-start(f32[10,1,256]{2,1,0:T(1,128)S(1)} %get-tuple-element.59), channel_id=1, source_target_pairs={{2,0},{4,2},{6,4},{3,1},{5,3},{7,5},{10,8},{12,10},{14,12},{11,9},... | collective-permute-start | bytes 30728 | tf_op jit(solution)/shard_map/ppermute | solution.py:24
  132.0 7.0 %collective-permute-start.33 = (f32[10,1,256]{2,1,0:T(1,128)S(1)}, f32[10,1,256]{2,1,0:T(1,128)S(1)}, u32[]{:S(2)}, u32[]{:S(2)}) collective-permute-start(f32[10,1,256]{2,1,0:T(1,128)S(1)} %get-tuple-element.58), channel_id=1, source_target_pairs={{0,2},{2,4},{4,6},{1,3},{3,5},{5,7},{8,10},{10,12},{12,14},{9,11},... | collective-permute-start | bytes 30728 | tf_op jit(solution)/shard_map/ppermute | solution.py:22
  184.8 10.4 %collective-permute-start.38 = (f32[10,1,256]{2,1,0:T(1,128)S(1)}, f32[10,1,256]{2,1,0:T(1,128)S(1)}, u32[]{:S(2)}, u32[]{:S(2)}) collective-permute-start(f32[10,1,256]{2,1,0:T(1,128)S(1)} %get-tuple-element.57), channel_id=1, source_target_pairs={{2,0},{4,2},{6,4},{3,1},{5,3},{7,5},{10,8},{12,10},{14,12},{11,9},... | collective-permute-start | bytes 30728 | tf_op jit(solution)/shard_map/ppermute | solution.py:24
  187.0 9.0 %collective-permute-start.39 = (f32[10,1,256]{2,1,0:T(1,128)S(1)}, f32[10,1,256]{2,1,0:T(1,128)S(1)}, u32[]{:S(2)}, u32[]{:S(2)}) collective-permute-start(f32[10,1,256]{2,1,0:T(1,128)S(1)} %get-tuple-element.56), channel_id=1, source_target_pairs={{0,2},{2,4},{4,6},{1,3},{3,5},{5,7},{8,10},{10,12},{12,14},{9,11},... | collective-permute-start | bytes 30728 | tf_op jit(solution)/shard_map/ppermute | solution.py:22
  210.3 8.1 %collective-permute-start.44 = (f32[10,1,256]{2,1,0:T(1,128)S(1)}, f32[10,1,256]{2,1,0:T(1,128)S(1)}, u32[]{:S(2)}, u32[]{:S(2)}) collective-permute-start(f32[10,1,256]{2,1,0:T(1,128)S(1)} %get-tuple-element.55), channel_id=1, source_target_pairs={{2,0},{4,2},{6,4},{3,1},{5,3},{7,5},{10,8},{12,10},{14,12},{11,9},... | collective-permute-start | bytes 30728 | tf_op jit(solution)/shard_map/ppermute | solution.py:24
  212.3 7.0 %collective-permute-start.45 = (f32[10,1,256]{2,1,0:T(1,128)S(1)}, f32[10,1,256]{2,1,0:T(1,128)S(1)}, u32[]{:S(2)}, u32[]{:S(2)}) collective-permute-start(f32[10,1,256]{2,1,0:T(1,128)S(1)} %get-tuple-element.54), channel_id=1, source_target_pairs={{0,2},{2,4},{4,6},{1,3},{3,5},{5,7},{8,10},{10,12},{12,14},{9,11},... | collective-permute-start | bytes 30728 | tf_op jit(solution)/shard_map/ppermute | solution.py:22
  233.6 8.0 %collective-permute-start.50 = (f32[10,1,256]{2,1,0:T(1,128)S(1)}, f32[10,1,256]{2,1,0:T(1,128)S(1)}, u32[]{:S(2)}, u32[]{:S(2)}) collective-permute-start(f32[10,1,256]{2,1,0:T(1,128)S(1)} %get-tuple-element.53), channel_id=1, source_target_pairs={{2,0},{4,2},{6,4},{3,1},{5,3},{7,5},{10,8},{12,10},{14,12},{11,9},... | collective-permute-start | bytes 30728 | tf_op jit(solution)/shard_map/ppermute | solution.py:24
  256.8 8.0 %collective-permute-start.56 = (f32[10,1,256]{2,1,0:T(1,128)S(1)}, f32[10,1,256]{2,1,0:T(1,128)S(1)}, u32[]{:S(2)}, u32[]{:S(2)}) collective-permute-start(f32[10,1,256]{2,1,0:T(1,128)S(1)} %get-tuple-element.51), channel_id=1, source_target_pairs={{2,0},{4,2},{6,4},{3,1},{5,3},{7,5},{10,8},{12,10},{14,12},{11,9},... | collective-permute-start | bytes 30728 | tf_op jit(solution)/shard_map/ppermute | solution.py:24
  (41 other events, 267.1 us)
where the time goes:
time: 279 us; the launch traced here: 274 us
  starting transfers between devices  194 us (70%)
  waiting for transfers between devices  36.9 us (13%)
  local copies, waits for them, and re-layouts  23.9 us (9%)
  other arithmetic  15.9 us (6%)
    ppermute x30, starting transfers between devices, padded_2(): lax.ppermute(tail, axis, [(i, (i + 1) % count) for i in range(ends)])  134 us
    ppermute x30, starting transfers between devices, padded_2(): lax.ppermute(head, axis, [((i + 1) % count, i) for i in range(ends)])  50.5 us
    ppermute x30, waiting for transfers between devices, padded_2(): lax.ppermute(tail, axis, [(i, (i + 1) % count) for i in range(ends)])  23.8 us
    reshape x2, local copies, waits for them, and re-layouts, block_mean(): values.reshape(extent[0] // 2, 2, extent[1] // 2, 2, extent[2] // 2, 2)  19.5 us
    reduce_sum x2, other arithmetic, block_mean(): values.reshape(extent[0] // 2, 2, extent[1] // 2, 2, extent[2] // 2, 2)  8.04 us
    ppermute x30, waiting for transfers between devices, padded_2(): lax.ppermute(head, axis, [((i + 1) % count, i) for i in range(ends)])  7.44 us
  transfers between devices with their start and end apart: 63, of which 33 were waited for; matrix products, arithmetic and copies ran while one was open for 6% of the time, Pallas kernels for 0%

commit v1 on v0

v1 whole, which is shorter than its diff:
```python
import functools

import jax
import jax.numpy as jnp
from jax import lax
from jax.experimental import pallas as pl
from jax.experimental.pallas import tpu as pltpu
from jax.sharding import PartitionSpec as P

CZ = 256
ROUNDS = 9
clog_factor = 0.2
shift_fine = 0.001
MESH = pl.DeviceIdType.MESH
AXES = ("gx", "gy", "gz")


def split3(x):
    hi = x.astype(jnp.bfloat16)
    rest = x - hi.astype(jnp.float32)
    mid = rest.astype(jnp.bfloat16)
    low = (rest - mid.astype(jnp.float32)).astype(jnp.bfloat16)
    return jnp.concatenate([hi, mid, low], axis=0)


def exact_dot(x, ones):
    rows = x.shape[0]
    y = jnp.dot(split3(x), ones, preferred_element_type=jnp.float32)
    return (y[2 * rows :] + y[rows : 2 * rows]) + y[:rows]


def kernel(
    sizes,
    src_hbm,
    con_hbm,
    msk_hbm,
    ids_hbm,
    out_ref,
    src,
    con,
    msk,
    ids,
    hx,
    hy,
    hz,
    sx,
    sy,
    sz,
    wx,
    wyi,
    wzi,
    wyh,
    wzh,
    diag,
    srd,
    tmp,
    pool_m,
    prol_m,
    cond_all,
    rhs_all,
    cond_send,
    rhs_send,
    fac,
    in_sem,
    send_sem,
    recv_sem,
    g_send,
    g_recv,
):
    X, Y, Z = src.shape
    ZC = Z // 2
    here = [lax.axis_index(a) for a in AXES]
    n_gz = sizes[2]
    length = n_gz * ZC
    stages = (length - 1).bit_length()

    loads = [
        pltpu.make_async_copy(a, b, in_sem.at[i])
        for i, (a, b) in enumerate(
            ((con_hbm, con), (msk_hbm, msk), (src_hbm, src), (ids_hbm, ids))
        )
    ]
    for load in loads:
        load.start()

    halo = (hx, hy, hz)
    outgoing = (sx, sy, sz)
    has = [
        (here[d] > 0, here[d] < sizes[d] - 1) for d in range(3)
    ]

    for d in range(3):
        for side in range(2):

            @pl.when(jnp.logical_not(has[d][side]))
            def _():
                for r in range(ROUNDS):
                    halo[d][r, side] = jnp.zeros(halo[d].shape[2:], jnp.float32)

    barrier = pltpu.get_barrier_semaphore()
    for d in range(2):
        for side in range(2):

            @pl.when(has[d][side])
            def _():
                pl.semaphore_signal(
                    barrier,
                    inc=1,
                    device_id={AXES[d]: here[d] + (2 * side - 1)},
                    device_id_type=MESH,
                )

    for off in range(1, n_gz):
        pl.semaphore_signal(
            barrier,
            inc=1,
            device_id={"gz": lax.rem(here[2] + off, n_gz)},
            device_id_type=MESH,
        )

    def face_copy(r, d, side):
        return pltpu.make_async_remote_copy(
            src_ref=outgoing[d].at[r, side],
            dst_ref=halo[d].at[r, 1 - side],
            send_sem=send_sem.at[r, d, side],
            recv_sem=recv_sem.at[r, d, 1 - side],
            device_id={AXES[d]: here[d] + (2 * side - 1)},
            device_id_type=MESH,
        )

    def face_arrival(r, d, side):
        return pltpu.make_async_remote_copy(
            src_ref=outgoing[d].at[r, side],
            dst_ref=halo[d].at[r, side],
            send_sem=send_sem.at[r, d, side],
            recv_sem=recv_sem.at[r, d, side],
            device_id={AXES[d]: here[d] + (2 * side - 1)},
            device_id_type=MESH,
        )

    lane = lax.broadcasted_iota(jnp.int32, (Y, 128), 1)

    def pack(p, side):
        at = Z - 1 if side else 0
        acc = jnp.broadcast_to(p[0, :, at : at + 1], (Y, 128))
        for x in range(1, X):
            acc = jnp.where(lane == x, jnp.broadcast_to(p[x, :, at : at + 1], (Y, 128)), acc)
        return acc

    def stage_faces(r, p):
        sx[r, 0] = p[0]
        sx[r, 1] = p[X - 1]
        sy[r, 0] = p[:, 0:1, :]
        sy[r, 1] = p[:, Y - 1 : Y, :]
        for side in range(2):

            @pl.when(has[2][side])
            def _():
                sz[r, side] = pack(p, side)

    def start_faces(r):
        for d in (2, 0, 1):
            for side in range(2):

                @pl.when(has[d][side])
                def _():
                    face_copy(r, d, side).start()

    def wait_faces(r):
        for d in range(3):
            for side in range(2):

                @pl.when(has[d][side])
                def _():
                    face_arrival(r, d, side).wait_recv()

    def send_faces(r, p):
        stage_faces(r, p)
        start_faces(r)

    def z_halo(r, side):
        packed = hz[r, side]
        return jnp.stack(
            [jnp.broadcast_to(packed[:, x : x + 1], (Y, 128)) for x in range(X)], axis=0
        )

    def gather_copy(buf, staged, which, off):
        return pltpu.make_async_remote_copy(
            src_ref=staged,
            dst_ref=buf.at[here[2]],
            send_sem=g_send.at[which, off - 1],
            recv_sem=g_recv.at[which, off - 1],
            device_id={"gz": lax.rem(here[2] + off, n_gz)},
            device_id_type=MESH,
        )

    def gather_start(buf, staged, which, value):
        staged[...] = value
        for off in range(1, n_gz):
            gather_copy(buf, staged, which, off).start()
        buf[here[2]] = value

    def gather_wait(buf, staged, which):
        for off in range(1, n_gz):
            gather_copy(buf, staged, which, off).wait_recv()
        return jnp.concatenate([buf[j] for j in range(n_gz)], axis=1)

    def pool(v):
        for h in range(2):
            part = v[:, :, 128 * h : 128 * h + 128].reshape(X // 2, 2, Y, 128)
            tmp[h] = (part[:, 0] + part[:, 1]).reshape(X // 2 * Y, 128)
        rows = X // 2 * Y // 2
        halves = [
            tmp[h, pl.ds(0, rows, stride=2), :] + tmp[h, pl.ds(1, rows, stride=2), :]
            for h in range(2)
        ]
        return exact_dot(jnp.concatenate(halves, axis=1), pool_m[...]) * 0.125

    loads[0].wait()
    loads[1].wait()
    c = con[...] * jnp.where(msk[...] > 0, clog_factor, 1.0)
    stage_faces(0, c)
    greeted = n_gz - 1
    for d in range(2):
        greeted = greeted + has[d][0].astype(jnp.int32) + has[d][1].astype(jnp.int32)
    pl.semaphore_wait(barrier, greeted)
    start_faces(0)

    k_of = lax.broadcasted_iota(jnp.int32, (Z, ZC), 0)
    j_of = lax.broadcasted_iota(jnp.int32, (Z, ZC), 1)
    pool_m[...] = jnp.where((k_of >> 1) == j_of, 1.0, 0.0).astype(jnp.bfloat16)
    k_of = lax.broadcasted_iota(jnp.int32, (ZC, Z), 1)
    j_of = lax.broadcasted_iota(jnp.int32, (ZC, Z), 0)
    prol_m[...] = jnp.where((k_of >> 1) == j_of, 1.0, 0.0).astype(jnp.bfloat16)
    gather_start(cond_all, cond_send, 0, pool(c))

    iy = lax.broadcasted_iota(jnp.int32, (X, Y, Z), 1)
    iz = lax.broadcasted_iota(jnp.int32, (X, Y, Z), 2)
    ix = lax.broadcasted_iota(jnp.int32, (X, Y, Z), 0)
    red = ((ix + iy + iz) & 1) == 0

    loads[2].wait()
    loads[3].wait()
    rows = X // 2 * Y // 2
    col = lax.broadcasted_iota(jnp.int32, (rows, ids.shape[3]), 0)
    hit = jnp.zeros((rows, ids.shape[3]), jnp.float32)
    for o in range(ids.shape[2]):
        hit = jnp.maximum(hit, jnp.where(ids[0, 0, o : o + 1, :] == col, 1.0, 0.0))
    flag = jnp.max(hit, axis=1, keepdims=True)

    wait_faces(0)
    xm = jnp.concatenate([hx[0, 0][None], c[:-1]], axis=0)
    xp = jnp.concatenate([c[1:], hx[0, 1][None]], axis=0)
    ym = jnp.where(iy == 0, jnp.broadcast_to(hy[0, 0], c.shape), pltpu.roll(c, 1, 1))
    yp = jnp.where(iy == Y - 1, jnp.broadcast_to(hy[0, 1], c.shape), pltpu.roll(c, Y - 1, 1))
    h0 = z_halo(0, 0)
    h1 = z_halo(0, 1)
    zm = jnp.where(iz == 0, jnp.concatenate([h0, h0], axis=2), pltpu.roll(c, 1, 2))
    zp = jnp.where(iz == Z - 1, jnp.concatenate([h1, h1], axis=2), pltpu.roll(c, Z - 1, 2))
    w = [0.5 * (c + beside) for beside in (xp, xm, yp, ym, zp, zm)]
    dg = shift_fine + w[0] + w[1] + w[2] + w[3] + w[4] + w[5]
    rd = 1.0 / dg
    s_rd = src[...] * rd
    p = jnp.where(red, s_rd, 0.0)
    send_faces(1, p)
    diag[...] = dg
    srd[...] = s_rd
    w = [one * rd for one in w]
    wx[0] = w[1]
    wx[1] = w[0]
    wyi[0] = jnp.where(iy == 0, 0.0, w[3])
    wyi[1] = jnp.where(iy == Y - 1, 0.0, w[2])
    wzi[0] = jnp.where(iz == 0, 0.0, w[5])
    wzi[1] = jnp.where(iz == Z - 1, 0.0, w[4])
    wyh[0] = jnp.where(iy == 0, w[3], 0.0)[:, :8]
    wyh[1] = jnp.where(iy == Y - 1, w[2], 0.0)[:, Y - 8 :]
    wzh[0] = jnp.where(iz == 0, w[5], 0.0)[:, :, :128]
    wzh[1] = jnp.where(iz == Z - 1, w[4], 0.0)[:, :, Z - 128 :]

    def interior(p):
        plane = jnp.zeros((1,) + p.shape[1:], jnp.float32)
        u = srd[...] + wx[0] * jnp.concatenate([plane, p[:-1]], axis=0)
        u = u + wx[1] * jnp.concatenate([p[1:], plane], axis=0)
        u = u + wyi[0] * pltpu.roll(p, 1, 1) + wyi[1] * pltpu.roll(p, Y - 1, 1)
        u = u + wzi[0] * pltpu.roll(p, 1, 2) + wzi[1] * pltpu.roll(p, Z - 1, 2)
        return u

    def with_halo(r, u):
        wait_faces(r)
        u = jnp.concatenate(
            [
                (u[0] + wx[0, 0] * hx[r, 0])[None],
                u[1:-1],
                (u[X - 1] + wx[1, X - 1] * hx[r, 1])[None],
            ],
            axis=0,
        )
        near = u[:, :8] + wyh[0] * jnp.broadcast_to(hy[r, 0], (X, 8, Z))
        far = u[:, Y - 8 :] + wyh[1] * jnp.broadcast_to(hy[r, 1], (X, 8, Z))
        u = jnp.concatenate([near, u[:, 8 : Y - 8], far] if Y > 16 else [near, far], axis=1)
        left = u[:, :, :128] + wzh[0] * z_halo(r, 0)
        right = u[:, :, Z - 128 :] + wzh[1] * z_halo(r, 1)
        return jnp.concatenate([left, right], axis=2)

    def factor(state, stage):
        lower, main, upper = state
        stride = 1 << stage
        rm = 1.0 / main
        low = -lower * pltpu.roll(rm, stride, 1)
        high = -upper * pltpu.roll(rm, length - stride, 1)
        fac[2 * stage] = low
        fac[2 * stage + 1] = high
        main = (
            main + low * pltpu.roll(upper, stride, 1) + high * pltpu.roll(lower, length - stride, 1)
        )
        lower = low * pltpu.roll(lower, stride, 1)
        upper = high * pltpu.roll(upper, length - stride, 1)
        return lower, main, upper

    u = interior(p)
    cond = gather_wait(cond_all, cond_send, 0)
    at = lax.broadcasted_iota(jnp.int32, cond.shape, 1)
    before = cond + pltpu.roll(cond, 1, 1)
    after = cond + pltpu.roll(cond, length - 1, 1)
    left_sum = jnp.where(at == 0, cond, before)
    right_sum = jnp.where(at == length - 1, cond, after)
    state = (
        jnp.where(at == 0, 0.0, -before),
        1.0 / (CZ * CZ) + left_sum + right_sum,
        jnp.where(at == length - 1, 0.0, -after),
    )
    per = -(-stages // 3)
    for stage in range(0, per):
        state = factor(state, stage)
    p = jnp.where(red, p, with_halo(1, u))
    send_faces(2, p)
    u = interior(p)
    for stage in range(per, min(2 * per, stages)):
        state = factor(state, stage)
    p = jnp.where(red, with_halo(2, u), p)
    send_faces(3, p)
    u = interior(p)
    for stage in range(2 * per, stages):
        state = factor(state, stage)
    fac[2 * stages] = (2.0 / (CZ * CZ)) / state[1]
    p = jnp.where(red, p, with_halo(3, u))
    send_faces(4, p)
    u = with_halo(4, interior(p))
    rhs = pool(diag[...] * (u - p)) * flag
    gather_start(rhs_all, rhs_send, 1, rhs)
    values = gather_wait(rhs_all, rhs_send, 1)
    for stage in range(stages):
        stride = 1 << stage
        values = (
            values
            + fac[2 * stage] * pltpu.roll(values, stride, 1)
            + fac[2 * stage + 1] * pltpu.roll(values, length - stride, 1)
        )
    rhs_all[...] = jnp.stack(
        [
            (values * fac[2 * stages])[:, ZC * j : ZC * j + ZC]
            for j in range(n_gz)
        ],
        axis=0,
    )
    mine = rhs_all[here[2]]
    fine = exact_dot(mine, prol_m[...])
    for h in range(2):
        part = fine[:, 128 * h : 128 * h + 128]
        tmp[h, pl.ds(0, rows, stride=2), :] = part
        tmp[h, pl.ds(1, rows, stride=2), :] = part
    add = jnp.concatenate([tmp[0], tmp[1]], axis=1).reshape(X // 2, 1, Y, Z)
    p = p + jnp.broadcast_to(add, (X // 2, 2, Y, Z)).reshape(X, Y, Z)

    for r in range(5, ROUNDS):
        send_faces(r, p)
        u = with_halo(r, interior(p))
        p = jnp.where(red, u, p) if r % 2 else jnp.where(red, p, u)
    out_ref[...] = p

    for r in range(ROUNDS):
        for d in range(3):
            for side in range(2):

                @pl.when(has[d][side])
                def _():
                    face_copy(r, d, side).wait_send()

    for off in range(1, n_gz):
        gather_copy(cond_all, cond_send, 0, off).wait_send()
        gather_copy(rhs_all, rhs_send, 1, off).wait_send()


def shards(sizes, source, conduct, solid_mask, line_ids):
    X, Y, Z = source.shape
    ZC = Z // 2
    rows = X // 2 * Y // 2
    n_gz = sizes[2]
    length = n_gz * ZC
    stages = (length - 1).bit_length()
    f32 = jnp.float32
    V = pltpu.VMEM
    dma = pltpu.SemaphoreType.DMA
    return pl.pallas_call(
        functools.partial(kernel, sizes),
        out_shape=jax.ShapeDtypeStruct((X, Y, Z), f32),
        in_specs=[pl.BlockSpec(memory_space=pl.ANY)] * 4,
        out_specs=pl.BlockSpec(memory_space=pltpu.VMEM),
        scratch_shapes=[
            V((X, Y, Z), f32),
            V((X, Y, Z), f32),
            V((X, Y, Z), jnp.int32),
            V(line_ids.shape, jnp.int32),
            V((ROUNDS, 2, Y, Z), f32),
            V((ROUNDS, 2, X, 1, Z), f32),
            V((ROUNDS, 2, Y, 128), f32),
            V((ROUNDS, 2, Y, Z), f32),
            V((ROUNDS, 2, X, 1, Z), f32),
            V((ROUNDS, 2, Y, 128), f32),
            V((2, X, Y, Z), f32),
            V((2, X, Y, Z), f32),
            V((2, X, Y, Z), f32),
            V((2, X, 8, Z), f32),
            V((2, X, Y, 128), f32),
            V((X, Y, Z), f32),
            V((X, Y, Z), f32),
            V((2, X // 2 * Y, 128), f32),
            V((Z, ZC), jnp.bfloat16),
            V((ZC, Z), jnp.bfloat16),
            V((n_gz, rows, ZC), f32),
            V((n_gz, rows, ZC), f32),
            V((rows, ZC), f32),
            V((rows, ZC), f32),
            V((2 * stages + 1, rows, length), f32),
            dma((4,)),
            dma((ROUNDS, 3, 2)),
            dma((ROUNDS, 3, 2)),
            dma((2, n_gz - 1)),
            dma((2, n_gz - 1)),
        ],
        compiler_params=pltpu.CompilerParams(
            collective_id=0, has_side_effects=True, vmem_limit_bytes=48 * 1024 * 1024
        ),
        name="cycle",
    )(source, conduct, solid_mask, line_ids)


def solution(mesh):
    sizes = tuple(mesh.shape[a] for a in AXES)
    in_specs = (
        P("gx", "gy", "gz"),
        P("gx", "gy", "gz"),
        P("gx", "gy", "gz"),
        P("gx", "gy", None, None),
    )
    out_specs = P("gx", "gy", "gz")
    return jax.shard_map(
        functools.partial(shards, sizes),
        mesh=mesh,
        in_specs=in_specs,
        out_specs=out_specs,
        check_vma=False,
    )
```

time: 279 us -> 40.5 us (0.15); the launches traced: 274 us -> 40.3 us
  starting transfers between devices: 194 us -> 0 us
  waiting for transfers between devices: 36.9 us -> 0 us
  Pallas kernels: 0 us -> 36.3 us
  local copies, waits for them, and re-layouts: 23.9 us -> 4.05 us
  other arithmetic: 15.9 us -> 0 us
    ppermute x60 -> x0, starting transfers between devices: 185 us -> none  [the longest x30 134 us: padded_2(): lax.ppermute(tail, axis, [(i, (i + 1) % count) for i in range(ends)])]
    pallas_call x0 -> x1, Pallas kernels: none -> 36.3 us  [shards(): pl.pallas_call(functools.partial(kernel, sizes), out_shape=jax.ShapeDtype...]
    ppermute x60 -> x0, waiting for transfers between devices: 31.2 us -> none  [the longest x30 23.8 us: padded_2(): lax.ppermute(tail, axis, [(i, (i + 1) % count) for i in range(ends)])]
    reshape x5 -> x0, local copies, waits for them, and re-layouts: 19.6 us -> none  [the longest x2 19.5 us: block_mean(): values.reshape(extent[0] // 2, 2, extent[1] // 2, 2, extent[2] // 2, 2)]
    all_to_all x3 -> x0, starting transfers between devices: 9.71 us -> none  [the longest x1 3.24 us: shards(): lax.all_to_all(send_cond, 'gz', split_axis=0, concat_axis=0, tiled=True)]
    reduce_sum x2 -> x0, other arithmetic: 8.04 us -> none  [block_mean(): values.reshape(extent[0] // 2, 2, extent[1] // 2, 2, extent[2] // 2, 2)]
    all_to_all x3 -> x0, waiting for transfers between devices: 5.62 us -> none  [the longest x1 3.02 us: shards(): lax.all_to_all(send_rhs, 'gz', split_axis=0, concat_axis=0, tiled=True)]
    select_n x8 -> x0, other arithmetic: 4.72 us -> none  [smoother(): pressure = jnp.where(colours == colour, updated, pressure)]
  transfers between devices with their start and end apart: 63 -> 0, of which waited for: 33 -> 0; matrix products, arithmetic and copies ran while one was open for 6% -> 0% of each run, Pallas kernels for 0% -> 0%
where the time goes in v1:
time: 40.5 us; the launch traced here: 40.3 us
  Pallas kernels  36.3 us (90%)
  local copies, waits for them, and re-layouts  4.05 us (10%)
    pallas_call x1, Pallas kernels, shards(): pl.pallas_call(functools.partial(kernel, sizes), out_shape=jax.ShapeDtype...  36.3 us
    unnamed x9, local copies, waits for them, and re-layouts  4.05 us

profile of v1, /device:TPU:1, one launch (start us, length us, event | category | flops | bytes accessed | tf_op | source)
XLA Modules:
  0.0 40.3 jit_solution(8558043927008210436)
XLA Ops:
  0.0 0.0 copy-start
  0.0 0.9 %copy-done = f32[8,16,256]{2,1,0:T(8,128)S(1)} copy-done((f32[8,16,256]{2,1,0:T(8,128)S(1)}, f32[8,16,256]{2,1,0:T(8,128)}, u32[]{:S(2)}) %copy-start) | copy-done | bytes 131096
  0.9 0.0 copy-start.1
  0.9 0.9 %copy-done.1 = f32[8,16,256]{2,1,0:T(8,128)S(1)} copy-done((f32[8,16,256]{2,1,0:T(8,128)S(1)}, f32[8,16,256]{2,1,0:T(8,128)}, u32[]{:S(2)}) %copy-start.1) | copy-done | bytes 131096
  1.8 0.0 copy-start.2
  1.8 0.9 %copy-done.2 = s32[8,16,256]{2,1,0:T(8,128)S(1)} copy-done((s32[8,16,256]{2,1,0:T(8,128)S(1)}, s32[8,16,256]{2,1,0:T(8,128)}, u32[]{:S(2)}) %copy-start.2) | copy-done | bytes 131096
  2.7 0.0 copy-start.3
  2.7 0.7 %copy-done.3 = s32[1,1,2,16]{3,2,1,0:T(2,128)S(1)} copy-done((s32[1,1,2,16]{3,2,1,0:T(2,128)S(1)}, s32[1,1,2,16]{3,2,1,0:T(2,128)}, u32[]{:S(2)}) %copy-start.3) | copy-done | bytes 152
  3.4 36.3 %cycle.1 = f32[8,16,256]{2,1,0:T(8,128)S(1)} custom-call(f32[8,16,256]{2,1,0:T(8,128)S(1)} %copy-done, f32[8,16,256]{2,1,0:T(8,128)S(1)} %copy-done.1, s32[8,16,256]{2,1,0:T(8,128)S(1)} %copy-done.2, s32[1,1,2,16]{3,2,1,0:T(2,128)S(1)} %copy-done.3), custom_call_target="tpu_custom_call" | custom-call | tf_op jit(solution)/shard_map/cycle/pallas_call | solution.py:404
  39.7 0.7 %copy.6 = f32[8,16,256]{2,1,0:T(8,128)} copy(f32[8,16,256]{2,1,0:T(8,128)S(1)} %cycle.1) | data formatting | bytes 262144
Async XLA Ops:
  0.0 0.9 %copy-start = (f32[8,16,256]{2,1,0:T(8,128)S(1)}, f32[8,16,256]{2,1,0:T(8,128)}, u32[]{:S(2)}) copy-start(f32[8,16,256]{2,1,0:T(8,128)} %src_hbm.1) | copy-start | bytes 393220
  0.9 0.9 %copy-start.1 = (f32[8,16,256]{2,1,0:T(8,128)S(1)}, f32[8,16,256]{2,1,0:T(8,128)}, u32[]{:S(2)}) copy-start(f32[8,16,256]{2,1,0:T(8,128)} %con_hbm.1) | copy-start | bytes 393220
  1.8 0.9 %copy-start.2 = (s32[8,16,256]{2,1,0:T(8,128)S(1)}, s32[8,16,256]{2,1,0:T(8,128)}, u32[]{:S(2)}) copy-start(s32[8,16,256]{2,1,0:T(8,128)} %msk_hbm.1) | copy-start | bytes 393220
  2.7 0.7 %copy-start.3 = (s32[1,1,2,16]{3,2,1,0:T(2,128)S(1)}, s32[1,1,2,16]{3,2,1,0:T(2,128)}, u32[]{:S(2)}) copy-start(s32[1,1,2,16]{3,2,1,0:T(2,128)} %ids_hbm.1) | copy-start | bytes 388

commit v2 on v1

v2 whole, which is shorter than its diff:
```python
import functools

import jax
import jax.numpy as jnp
from jax import lax
from jax.experimental import pallas as pl
from jax.experimental.pallas import tpu as pltpu
from jax.sharding import PartitionSpec as P

CZ = 256
CHANNELS = 7
EDGES = ((0, 1), (0, 2), (1, 2))
clog_factor = 0.2
shift_fine = 0.001
MESH = pl.DeviceIdType.MESH
AXES = ("gx", "gy", "gz")


def split3(x):
    hi = x.astype(jnp.bfloat16)
    rest = x - hi.astype(jnp.float32)
    mid = rest.astype(jnp.bfloat16)
    low = (rest - mid.astype(jnp.float32)).astype(jnp.bfloat16)
    return jnp.concatenate([hi, mid, low], axis=0)


def exact_dot(x, ones):
    rows = x.shape[0]
    y = jnp.dot(split3(x), ones, preferred_element_type=jnp.float32)
    return (y[2 * rows :] + y[rows : 2 * rows]) + y[:rows]


def kernel(
    sizes,
    src_hbm,
    con_hbm,
    msk_hbm,
    ids_hbm,
    out_ref,
    src,
    con,
    msk,
    ids,
    hx,
    hy,
    hz,
    sx,
    sy,
    sz,
    hxy,
    hxz,
    hyz,
    wts,
    diag,
    srd,
    tmp,
    pool_m,
    prol_m,
    cond_all,
    rhs_all,
    cond_send,
    rhs_send,
    fac,
    in_sem,
    send_sem,
    recv_sem,
    g_send,
    g_recv,
):
    X, Y, Z = src.shape
    ZC = Z // 2
    here = [lax.axis_index(a) for a in AXES]
    n_gz = sizes[2]
    length = n_gz * ZC
    stages = (length - 1).bit_length()

    loads = [
        pltpu.make_async_copy(a, b, in_sem.at[i])
        for i, (a, b) in enumerate(
            ((con_hbm, con), (msk_hbm, msk), (src_hbm, src), (ids_hbm, ids))
        )
    ]
    for load in loads:
        load.start()

    halo = (hx, hy, hz)
    outgoing = (sx, sy, sz)
    edge_halo = (hxy, hxz, hyz)
    has = [(here[d] > 0, here[d] < sizes[d] - 1) for d in range(3)]

    def beside(d, side):
        return {AXES[d]: here[d] + (2 * side - 1)}

    faces = [(d, side) for d in (2, 0, 1) for side in range(2)]
    edges = [(e, a, b) for e in range(3) for a in range(2) for b in range(2)]

    def has_edge(e, a, b):
        return jnp.logical_and(has[EDGES[e][0]][a], has[EDGES[e][1]][b])

    for d, side in faces:

        @pl.when(jnp.logical_not(has[d][side]))
        def _():
            for r in range(CHANNELS):
                halo[d][r, side] = jnp.zeros(halo[d].shape[2:], jnp.float32)

    for e, a, b in edges:

        @pl.when(jnp.logical_not(has_edge(e, a, b)))
        def _():
            for r in (0, 3, 5, 6):
                edge_halo[e][r, a, b] = jnp.zeros(edge_halo[e].shape[3:], jnp.float32)

    barrier = pltpu.get_barrier_semaphore()
    greeted = n_gz - 1
    for d, side in faces:
        if d == 2:
            continue
        greeted = greeted + has[d][side].astype(jnp.int32)

        @pl.when(has[d][side])
        def _():
            pl.semaphore_signal(
                barrier, inc=1, device_id=beside(d, side), device_id_type=MESH
            )

    for e, a, b in edges:
        greeted = greeted + has_edge(e, a, b).astype(jnp.int32)

        @pl.when(has_edge(e, a, b))
        def _():
            pl.semaphore_signal(
                barrier,
                inc=1,
                device_id={**beside(EDGES[e][0], a), **beside(EDGES[e][1], b)},
                device_id_type=MESH,
            )

    for off in range(1, n_gz):
        pl.semaphore_signal(
            barrier,
            inc=1,
            device_id={"gz": lax.rem(here[2] + off, n_gz)},
            device_id_type=MESH,
        )

    def channels_of(ch):
        return pl.ds(0, 3) if ch == 0 else ch

    def face_copy(ch, d, side, parity, arrival=False):
        at = side if arrival else 1 - side
        return pltpu.make_async_remote_copy(
            src_ref=outgoing[d].at[channels_of(ch), side],
            dst_ref=halo[d].at[channels_of(ch), at],
            send_sem=send_sem.at[2 * d + side],
            recv_sem=recv_sem.at[parity, 2 * d + at],
            device_id=beside(d, side),
            device_id_type=MESH,
        )

    def edge_copy(ch, e, a, b, parity, arrival=False):
        to = (a, b) if arrival else (1 - a, 1 - b)
        if e == 0:
            piece = sy.at[ch, b, a * (X - 1)]
        elif e == 1:
            piece = sz.at[ch, b]
        else:
            piece = sz.at[ch, b, pl.ds(a * (Y - 8), 8)]
        return pltpu.make_async_remote_copy(
            src_ref=piece,
            dst_ref=edge_halo[e].at[ch, to[0], to[1]],
            send_sem=send_sem.at[6 + 4 * e + 2 * a + b],
            recv_sem=recv_sem.at[parity, 6 + 4 * e + 2 * to[0] + to[1]],
            device_id={**beside(EDGES[e][0], a), **beside(EDGES[e][1], b)},
            device_id_type=MESH,
        )

    lane = lax.broadcasted_iota(jnp.int32, (Y, 128), 1)
    sub_y = lax.broadcasted_iota(jnp.int32, (X, 8, Z), 1)
    lane_z = lax.broadcasted_iota(jnp.int32, (X, Y, 128), 2)
    iy = lax.broadcasted_iota(jnp.int32, (X, Y, Z), 1)
    iz = lax.broadcasted_iota(jnp.int32, (X, Y, Z), 2)
    ix = lax.broadcasted_iota(jnp.int32, (X, Y, Z), 0)
    red = ((ix + iy + iz) & 1) == 0
    wide = (X + 2, Y + 8, Z + 128)
    red_wide = (
        (
            lax.broadcasted_iota(jnp.int32, wide, 0)
            + lax.broadcasted_iota(jnp.int32, wide, 1)
            + lax.broadcasted_iota(jnp.int32, wide, 2)
        )
        & 1
    ) == 1

    def pack(tile, at):
        acc = jnp.broadcast_to(tile[0, :, at : at + 1], (Y, 128))
        for x in range(1, X):
            acc = jnp.where(lane == x, jnp.broadcast_to(tile[x, :, at : at + 1], (Y, 128)), acc)
        return acc

    def stage_layer(ch, p, k):
        sx[ch, 0] = p[k]
        sx[ch, 1] = p[X - 1 - k]
        sy[ch, 0] = p[:, k : k + 1, :]
        sy[ch, 1] = p[:, Y - 1 - k : Y - k, :]

        @pl.when(has[2][0])
        def _():
            sz[ch, 0] = pack(p[:, :, :128], k)

        @pl.when(has[2][1])
        def _():
            sz[ch, 1] = pack(p[:, :, Z - 128 :], 127 - k)

    def stage_black(ch, p):
        sx[ch, 0] = jnp.where(red[0], p[1], p[0])
        sx[ch, 1] = jnp.where(red[X - 1], p[X - 2], p[X - 1])
        low = p[:, :8]
        sy[ch, 0] = jnp.where(red[:, :8], pltpu.roll(low, 7, 1), low)[:, 0:1, :]
        high = p[:, Y - 8 :]
        sy[ch, 1] = jnp.where(red[:, Y - 8 :], pltpu.roll(high, 1, 1), high)[:, 7:8, :]

        @pl.when(has[2][0])
        def _():
            t = p[:, :, :128]
            sz[ch, 0] = pack(jnp.where(red[:, :, :128], pltpu.roll(t, 127, 2), t), 0)

        @pl.when(has[2][1])
        def _():
            t = p[:, :, Z - 128 :]
            sz[ch, 1] = pack(jnp.where(red[:, :, Z - 128 :], pltpu.roll(t, 1, 2), t), 127)

    def start(ch, parity, edge_parity):
        if edge_parity is not None:
            for e, a, b in edges:

                @pl.when(has_edge(e, a, b))
                def _():
                    edge_copy(ch, e, a, b, edge_parity).start()

        for d, side in faces:

            @pl.when(has[d][side])
            def _():
                face_copy(ch, d, side, parity).start()

    def finish(ch, parity, edge_parity):
        for d, side in faces:

            @pl.when(has[d][side])
            def _():
                face_copy(ch, d, side, parity, True).wait_recv()
                face_copy(ch, d, side, parity).wait_send()

        if edge_parity is not None:
            for e, a, b in edges:

                @pl.when(has_edge(e, a, b))
                def _():
                    edge_copy(ch, e, a, b, edge_parity, True).wait_recv()
                    edge_copy(ch, e, a, b, edge_parity).wait_send()

    def columns(packed, xs):
        return jnp.stack(
            [jnp.broadcast_to(packed[:, x : x + 1], (packed.shape[0], 128)) for x in xs], axis=0
        )

    near_y = sub_y < 4
    near_z = lane_z < 64

    def widen(p, ch, with_edges, second=None):
        y_plus = jnp.broadcast_to(hy[ch, 1], (X, 8, Z))
        y_minus = jnp.broadcast_to(hy[ch, 0], (X, 8, Z))
        z_plus = columns(hz[ch, 1], range(X))
        z_minus = columns(hz[ch, 0], range(X))
        if second is None:
            ytile = jnp.where(near_y, y_plus, y_minus)
            ztile = jnp.where(near_z, z_plus, z_minus)
        else:
            y_plus2 = jnp.broadcast_to(hy[second, 1], (X, 8, Z))
            y_minus2 = jnp.broadcast_to(hy[second, 0], (X, 8, Z))
            z_plus2 = columns(hz[second, 1], range(X))
            z_minus2 = columns(hz[second, 0], range(X))
            ytile = jnp.where(
                near_y,
                jnp.where(sub_y == 0, y_plus, y_plus2),
                jnp.where(sub_y == 7, y_minus, y_minus2),
            )
            ztile = jnp.where(
                near_z,
                jnp.where(lane_z == 0, z_plus, z_plus2),
                jnp.where(lane_z == 127, z_minus, z_minus2),
            )
        if with_edges:
            yz = []
            for side in range(2):
                rows8 = jnp.where(near_y[0, :, :128], hyz[ch, 1, side], hyz[ch, 0, side])
                yz.append(columns(rows8, range(X)))
            yztile = jnp.where(near_z[:, :8], yz[1], yz[0])
        else:
            yztile = jnp.zeros((X, 8, 128), jnp.float32)
        top = jnp.concatenate([p, ztile], axis=2)
        core = jnp.concatenate([top, jnp.concatenate([ytile, yztile], axis=2)], axis=1)
        planes = []
        for side in range(2):
            if with_edges:
                xy = jnp.where(
                    near_y[0],
                    jnp.broadcast_to(hxy[ch, side, 1], (8, Z)),
                    jnp.broadcast_to(hxy[ch, side, 0], (8, Z)),
                )
                at = 0 if side else X - 1
                xz = jnp.where(
                    near_z[0],
                    columns(hxz[ch, side, 1], (at,))[0],
                    columns(hxz[ch, side, 0], (at,))[0],
                )
            else:
                xy = jnp.zeros((8, Z), jnp.float32)
                xz = jnp.zeros((Y, 128), jnp.float32)
            first = jnp.concatenate([hx[ch, side], xz], axis=1)
            last = jnp.concatenate([xy, jnp.zeros((8, 128), jnp.float32)], axis=1)
            planes.append(jnp.concatenate([first, last], axis=0)[None])
        return jnp.concatenate([planes[0], core, planes[1]], axis=0)

    def around(v, lowest, highest):
        return (
            jnp.concatenate([v[1:], highest], axis=0),
            jnp.concatenate([lowest, v[:-1]], axis=0),
            pltpu.roll(v, Y + 7, 1),
            pltpu.roll(v, 1, 1),
            pltpu.roll(v, Z + 127, 2),
            pltpu.roll(v, 1, 2),
        )

    def wide_update(v):
        u = srd[...]
        for i, one in enumerate(around(v, v[:1], v[X + 1 :])):
            u = u + wts[i] * one
        return u

    def own(v):
        return v[1 : X + 1, :Y, :Z]

    def own_update(v):
        besides = (
            v[2:, :Y, :Z],
            v[:X, :Y, :Z],
            pltpu.roll(v[1 : X + 1, :, :Z], Y + 7, 1)[:, :Y],
            pltpu.roll(v[1 : X + 1, :, :Z], 1, 1)[:, :Y],
            pltpu.roll(v[1 : X + 1, :Y], Z + 127, 2)[:, :, :Z],
            pltpu.roll(v[1 : X + 1, :Y], 1, 2)[:, :, :Z],
        )
        u = srd[1 : X + 1, :Y, :Z]
        for i, one in enumerate(besides):
            u = u + wts[i, 1 : X + 1, :Y, :Z] * one
        return u

    def sweep(p, ch):
        v = widen(p, ch, True)
        v = jnp.where(red_wide, wide_update(v), v)
        return jnp.where(red, own(v), own_update(v))

    def gather_copy(buf, staged, which, off):
        return pltpu.make_async_remote_copy(
            src_ref=staged,
            dst_ref=buf.at[here[2]],
            send_sem=g_send.at[which, off - 1],
            recv_sem=g_recv.at[which, off - 1],
            device_id={"gz": lax.rem(here[2] + off, n_gz)},
            device_id_type=MESH,
        )

    def gather_start(buf, staged, which, value):
        staged[...] = value
        for off in range(1, n_gz):
            gather_copy(buf, staged, which, off).start()
        buf[here[2]] = value

    def gather_wait(buf, staged, which):
        for off in range(1, n_gz):
            gather_copy(buf, staged, which, off).wait_recv()
        return jnp.concatenate([buf[j] for j in range(n_gz)], axis=1)

    def pool(v):
        for h in range(2):
            part = v[:, :, 128 * h : 128 * h + 128].reshape(X // 2, 2, Y, 128)
            tmp[h] = (part[:, 0] + part[:, 1]).reshape(X // 2 * Y, 128)
        rows = X // 2 * Y // 2
        halves = [
            tmp[h, pl.ds(0, rows, stride=2), :] + tmp[h, pl.ds(1, rows, stride=2), :]
            for h in range(2)
        ]
        return exact_dot(jnp.concatenate(halves, axis=1), pool_m[...]) * 0.125

    loads[0].wait()
    loads[1].wait()
    c = con[...] * jnp.where(msk[...] > 0, clog_factor, 1.0)
    stage_layer(0, c, 0)
    stage_layer(1, c, 1)
    loads[2].wait()
    loads[3].wait()
    stage_layer(2, src[...], 0)
    pl.semaphore_wait(barrier, greeted)
    start(0, 0, 0)

    k_of = lax.broadcasted_iota(jnp.int32, (Z, ZC), 0)
    j_of = lax.broadcasted_iota(jnp.int32, (Z, ZC), 1)
    pool_m[...] = jnp.where((k_of >> 1) == j_of, 1.0, 0.0).astype(jnp.bfloat16)
    k_of = lax.broadcasted_iota(jnp.int32, (ZC, Z), 1)
    j_of = lax.broadcasted_iota(jnp.int32, (ZC, Z), 0)
    prol_m[...] = jnp.where((k_of >> 1) == j_of, 1.0, 0.0).astype(jnp.bfloat16)
    gather_start(cond_all, cond_send, 0, pool(c))

    rows = X // 2 * Y // 2
    col = lax.broadcasted_iota(jnp.int32, (rows, ids.shape[3]), 0)
    hit = jnp.zeros((rows, ids.shape[3]), jnp.float32)
    for o in range(ids.shape[2]):
        hit = jnp.maximum(hit, jnp.where(ids[0, 0, o : o + 1, :] == col, 1.0, 0.0))
    flag = jnp.max(hit, axis=1, keepdims=True)

    finish(0, 0, 0)
    cw = widen(c, 0, True, 1)
    pad = jnp.zeros((Y, 128), jnp.float32)
    second = [
        jnp.concatenate(
            [
                jnp.concatenate([hx[1, side], pad], axis=1),
                jnp.zeros((8, Z + 128), jnp.float32),
            ],
            axis=0,
        )[None]
        for side in range(2)
    ]
    w = [0.5 * (cw + one) for one in around(cw, second[0], second[1])]
    dg = shift_fine + w[0] + w[1] + w[2] + w[3] + w[4] + w[5]
    rd = jnp.where(cw > 0.0, 1.0 / dg, 0.0)
    diag[...] = own(dg)
    v = widen(src[...], 2, False) * rd
    srd[...] = v
    for i in range(6):
        wts[i] = w[i] * rd
    v = jnp.where(red_wide, v, 0.0)
    p = jnp.where(red, own(v), own_update(v))
    stage_black(3, p)
    start(3, 1, 1)

    def factor(state, stage):
        lower, main, upper = state
        stride = 1 << stage
        rm = 1.0 / main
        low = -lower * pltpu.roll(rm, stride, 1)
        high = -upper * pltpu.roll(rm, length - stride, 1)
        fac[2 * stage] = low
        fac[2 * stage + 1] = high
        main = (
            main + low * pltpu.roll(upper, stride, 1) + high * pltpu.roll(lower, length - stride, 1)
        )
        lower = low * pltpu.roll(lower, stride, 1)
        upper = high * pltpu.roll(upper, length - stride, 1)
        return lower, main, upper

    cond = gather_wait(cond_all, cond_send, 0)
    at = lax.broadcasted_iota(jnp.int32, cond.shape, 1)
    before = cond + pltpu.roll(cond, 1, 1)
    after = cond + pltpu.roll(cond, length - 1, 1)
    left_sum = jnp.where(at == 0, cond, before)
    right_sum = jnp.where(at == length - 1, cond, after)
    state = (
        jnp.where(at == 0, 0.0, -before),
        1.0 / (CZ * CZ) + left_sum + right_sum,
        jnp.where(at == length - 1, 0.0, -after),
    )
    per = stages // 2
    for stage in range(0, per):
        state = factor(state, stage)
    finish(3, 1, 1)
    p = sweep(p, 3)
    stage_black(4, p)
    start(4, 0, None)
    for stage in range(per, stages):
        state = factor(state, stage)
    fac[2 * stages] = (2.0 / (CZ * CZ)) / state[1]
    finish(4, 0, None)
    u = own_update(widen(p, 4, False))
    rhs = pool(jnp.where(red, diag[...] * (u - p), 0.0)) * flag
    gather_start(rhs_all, rhs_send, 1, rhs)
    values = gather_wait(rhs_all, rhs_send, 1)
    for stage in range(stages):
        stride = 1 << stage
        values = (
            values
            + fac[2 * stage] * pltpu.roll(values, stride, 1)
            + fac[2 * stage + 1] * pltpu.roll(values, length - stride, 1)
        )
    rhs_all[...] = jnp.stack(
        [
            (values * fac[2 * stages])[:, ZC * j : ZC * j + ZC]
            for j in range(n_gz)
        ],
        axis=0,
    )
    mine = rhs_all[here[2]]
    fine = exact_dot(mine, prol_m[...])
    for h in range(2):
        part = fine[:, 128 * h : 128 * h + 128]
        tmp[h, pl.ds(0, rows, stride=2), :] = part
        tmp[h, pl.ds(1, rows, stride=2), :] = part
    add = jnp.concatenate([tmp[0], tmp[1]], axis=1).reshape(X // 2, 1, Y, Z)
    p = p + jnp.broadcast_to(add, (X // 2, 2, Y, Z)).reshape(X, Y, Z)

    stage_black(5, p)
    start(5, 1, 0)
    finish(5, 1, 0)
    p = sweep(p, 5)
    stage_black(6, p)
    start(6, 0, 1)
    finish(6, 0, 1)
    out_ref[...] = sweep(p, 6)

    for off in range(1, n_gz):
        gather_copy(cond_all, cond_send, 0, off).wait_send()
        gather_copy(rhs_all, rhs_send, 1, off).wait_send()


def shards(sizes, source, conduct, solid_mask, line_ids):
    X, Y, Z = source.shape
    ZC = Z // 2
    rows = X // 2 * Y // 2
    n_gz = sizes[2]
    length = n_gz * ZC
    stages = (length - 1).bit_length()
    f32 = jnp.float32
    V = pltpu.VMEM
    dma = pltpu.SemaphoreType.DMA
    return pl.pallas_call(
        functools.partial(kernel, sizes),
        out_shape=jax.ShapeDtypeStruct((X, Y, Z), f32),
        in_specs=[pl.BlockSpec(memory_space=pltpu.HBM)] * 4,
        out_specs=pl.BlockSpec(memory_space=pltpu.VMEM),
        scratch_shapes=[
            V((X, Y, Z), f32),
            V((X, Y, Z), f32),
            V((X, Y, Z), jnp.int32),
            V(line_ids.shape, jnp.int32),
            V((CHANNELS, 2, Y, Z), f32),
            V((CHANNELS, 2, X, 1, Z), f32),
            V((CHANNELS, 2, Y, 128), f32),
            V((CHANNELS, 2, Y, Z), f32),
            V((CHANNELS, 2, X, 1, Z), f32),
            V((CHANNELS, 2, Y, 128), f32),
            V((CHANNELS, 2, 2, 1, Z), f32),
            V((CHANNELS, 2, 2, Y, 128), f32),
            V((CHANNELS, 2, 2, 8, 128), f32),
            V((6, X + 2, Y + 8, Z + 128), f32),
            V((X, Y, Z), f32),
            V((X + 2, Y + 8, Z + 128), f32),
            V((2, X // 2 * Y, 128), f32),
            V((Z, ZC), jnp.bfloat16),
            V((ZC, Z), jnp.bfloat16),
            V((n_gz, rows, ZC), f32),
            V((n_gz, rows, ZC), f32),
            V((rows, ZC), f32),
            V((rows, ZC), f32),
            V((2 * stages + 1, rows, length), f32),
            dma((4,)),
            dma((18,)),
            dma((2, 18)),
            dma((2, n_gz - 1)),
            dma((2, n_gz - 1)),
        ],
        compiler_params=pltpu.CompilerParams(
            collective_id=0, has_side_effects=True, vmem_limit_bytes=67043328
        ),
        name="cycle",
    )(source, conduct, solid_mask, line_ids)


def solution(mesh):
    sizes = tuple(mesh.shape[a] for a in AXES)
    in_specs = (
        P("gx", "gy", "gz"),
        P("gx", "gy", "gz"),
        P("gx", "gy", "gz"),
        P("gx", "gy", None, None),
    )
    out_specs = P("gx", "gy", "gz")
    return jax.shard_map(
        functools.partial(shards, sizes),
        mesh=mesh,
        in_specs=in_specs,
        out_specs=out_specs,
        check_vma=False,
    )
```

time: 40.5 us -> 30.4 us (0.75)
  Pallas kernels: 36.3 us -> 28.6 us
  local copies, waits for them, and re-layouts: 4.05 us -> 1.57 us
    pallas_call x1, Pallas kernels: 36.3 us -> 28.6 us  [shards(): pl.pallas_call(functools.partial(kernel, sizes), out_shape=jax.ShapeDtype...]
    unnamed x9 -> x1, local copies, waits for them, and re-layouts: 4.05 us -> 1.57 us
where the time goes in v2:
time: 30.4 us; the launch traced here: 30.2 us
  Pallas kernels  28.6 us (94%)
  local copies, waits for them, and re-layouts  1.57 us (5%)
    pallas_call x1, Pallas kernels, shards(): pl.pallas_call(functools.partial(kernel, sizes), out_shape=jax.ShapeDtype...  28.6 us
    unnamed x1, local copies, waits for them, and re-layouts  1.57 us

profile of v2, /device:TPU:1, one launch (start us, length us, event | category | flops | bytes accessed | tf_op | source)
XLA Modules:
  0.0 30.2 jit_solution(14841348238148383180)
XLA Ops:
  0.0 28.6 %cycle.1 = f32[8,16,256]{2,1,0:T(8,128)} custom-call(f32[8,16,256]{2,1,0:T(8,128)} %src_hbm.1, f32[8,16,256]{2,1,0:T(8,128)} %con_hbm.1, s32[8,16,256]{2,1,0:T(8,128)} %msk_hbm.1, s32[1,1,2,16]{3,2,1,0:T(2,128)} %ids_hbm.1), custom_call_target="tpu_custom_call" | custom-call | tf_op jit(solution)/shard_map/cycle/pallas_call | solution.py:536
  28.7 1.6 %copy.6 = f32[8,16,256]{2,1,0:T(8,128)} copy(f32[8,16,256]{2,1,0:T(8,128)} %cycle.1) | data formatting | bytes 262144

commit v3 on v2

--- a/solution.py
+++ b/solution.py
@@ -51,6 +51,8 @@
     hxz,
     hyz,
     wts,
+    field,
+    after,
     diag,
     srd,
     tmp,
@@ -183,15 +185,6 @@
     ix = lax.broadcasted_iota(jnp.int32, (X, Y, Z), 0)
     red = ((ix + iy + iz) & 1) == 0
     wide = (X + 2, Y + 8, Z + 128)
-    red_wide = (
-        (
-            lax.broadcasted_iota(jnp.int32, wide, 0)
-            + lax.broadcasted_iota(jnp.int32, wide, 1)
-            + lax.broadcasted_iota(jnp.int32, wide, 2)
-        )
-        & 1
-    ) == 1
-
     def pack(tile, at):
         acc = jnp.broadcast_to(tile[0, :, at : at + 1], (Y, 128))
         for x in range(1, X):
@@ -323,43 +316,59 @@
             planes.append(jnp.concatenate([first, last], axis=0)[None])
         return jnp.concatenate([planes[0], core, planes[1]], axis=0)
 
-    def around(v, lowest, highest):
+    line_of = lax.broadcasted_iota(jnp.int32, wide[1:], 0)
+    cell_of = lax.broadcasted_iota(jnp.int32, wide[1:], 1)
+    odd = ((line_of + cell_of) & 1) == 1
+    reds = (odd, jnp.logical_not(odd))
+
+    def around(v, low, high):
         return (
-            jnp.concatenate([v[1:], highest], axis=0),
-            jnp.concatenate([lowest, v[:-1]], axis=0),
-            pltpu.roll(v, Y + 7, 1),
+            high,
+            low,
+            pltpu.roll(v, Y + 7, 0),
+            pltpu.roll(v, 1, 0),
+            pltpu.roll(v, Z + 127, 1),
             pltpu.roll(v, 1, 1),
-            pltpu.roll(v, Z + 127, 2),
-            pltpu.roll(v, 1, 2),
-        )
-
-    def wide_update(v):
-        u = srd[...]
-        for i, one in enumerate(around(v, v[:1], v[X + 1 :])):
-            u = u + wts[i] * one
+        )
+
+    def own_plane(field, i):
+        besides = (
+            field[min(i + 1, X + 1), :Y, :Z],
+            field[max(i - 1, 0), :Y, :Z],
+            pltpu.roll(field[i, :, :Z], Y + 7, 0)[:Y],
+            pltpu.roll(field[i, :, :Z], 1, 0)[:Y],
+            pltpu.roll(field[i, :Y, :], Z + 127, 1)[:, :Z],
+            pltpu.roll(field[i, :Y, :], 1, 1)[:, :Z],
+        )
+        u = srd[i, :Y, :Z]
+        for k, one in enumerate(besides):
+            u = u + wts[k, i, :Y, :Z] * one
         return u
 
-    def own(v):
-        return v[1 : X + 1, :Y, :Z]
-
-    def own_update(v):
-        besides = (
-            v[2:, :Y, :Z],
-            v[:X, :Y, :Z],
-            pltpu.roll(v[1 : X + 1, :, :Z], Y + 7, 1)[:, :Y],
-            pltpu.roll(v[1 : X + 1, :, :Z], 1, 1)[:, :Y],
-            pltpu.roll(v[1 : X + 1, :Y], Z + 127, 2)[:, :, :Z],
-            pltpu.roll(v[1 : X + 1, :Y], 1, 2)[:, :, :Z],
-        )
-        u = srd[1 : X + 1, :Y, :Z]
-        for i, one in enumerate(besides):
-            u = u + wts[i, 1 : X + 1, :Y, :Z] * one
-        return u
+    def black_update():
+        return jnp.stack(
+            [
+                jnp.where(reds[i % 2][:Y, :Z], after[i, :Y, :Z], own_plane(after, i))
+                for i in range(1, X + 1)
+            ],
+            axis=0,
+        )
 
     def sweep(p, ch):
-        v = widen(p, ch, True)
-        v = jnp.where(red_wide, wide_update(v), v)
-        return jnp.where(red, own(v), own_update(v))
+        field[...] = widen(p, ch, True)
+        for i in range(X + 2):
+            mask = reds[i % 2]
+            if i in (0, X + 1):
+                after[i, :Y, :Z] = jnp.where(
+                    mask[:Y, :Z], own_plane(field, i), field[i, :Y, :Z]
+                )
+            else:
+                v = field[i]
+                u = srd[i]
+                for k, one in enumerate(around(v, field[i - 1], field[i + 1])):
+                    u = u + wts[k, i] * one
+                after[i] = jnp.where(mask, u, v)
+        return black_update()
 
     def gather_copy(buf, staged, which, off):
         return pltpu.make_async_remote_copy(
@@ -420,28 +429,33 @@
     flag = jnp.max(hit, axis=1, keepdims=True)
 
     finish(0, 0, 0)
-    cw = widen(c, 0, True, 1)
-    pad = jnp.zeros((Y, 128), jnp.float32)
+    field[...] = widen(c, 0, True, 1)
+    after[...] = widen(src[...], 2, False)
     second = [
         jnp.concatenate(
             [
-                jnp.concatenate([hx[1, side], pad], axis=1),
+                jnp.concatenate([hx[1, side], jnp.zeros((Y, 128), jnp.float32)], axis=1),
                 jnp.zeros((8, Z + 128), jnp.float32),
             ],
             axis=0,
-        )[None]
+        )
         for side in range(2)
     ]
-    w = [0.5 * (cw + one) for one in around(cw, second[0], second[1])]
-    dg = shift_fine + w[0] + w[1] + w[2] + w[3] + w[4] + w[5]
-    rd = jnp.where(cw > 0.0, 1.0 / dg, 0.0)
-    diag[...] = own(dg)
-    v = widen(src[...], 2, False) * rd
-    srd[...] = v
-    for i in range(6):
-        wts[i] = w[i] * rd
-    v = jnp.where(red_wide, v, 0.0)
-    p = jnp.where(red, own(v), own_update(v))
+    for i in range(X + 2):
+        v = field[i]
+        low = field[i - 1] if i else second[0]
+        high = field[i + 1] if i < X + 1 else second[1]
+        w = [0.5 * (v + one) for one in around(v, low, high)]
+        dg = shift_fine + w[0] + w[1] + w[2] + w[3] + w[4] + w[5]
+        rd = jnp.where(v > 0.0, 1.0 / dg, 0.0)
+        if 0 < i < X + 1:
+            diag[i - 1] = dg[:Y, :Z]
+        for k in range(6):
+            wts[k, i] = w[k] * rd
+        v = after[i] * rd
+        srd[i] = v
+        after[i] = jnp.where(reds[i % 2], v, 0.0)
+    p = black_update()
     stage_black(3, p)
     start(3, 1, 1)
 
@@ -462,14 +476,14 @@
 
     cond = gather_wait(cond_all, cond_send, 0)
     at = lax.broadcasted_iota(jnp.int32, cond.shape, 1)
-    before = cond + pltpu.roll(cond, 1, 1)
-    after = cond + pltpu.roll(cond, length - 1, 1)
-    left_sum = jnp.where(at == 0, cond, before)
-    right_sum = jnp.where(at == length - 1, cond, after)
+    sum_low = cond + pltpu.roll(cond, 1, 1)
+    sum_high = cond + pltpu.roll(cond, length - 1, 1)
+    left_sum = jnp.where(at == 0, cond, sum_low)
+    right_sum = jnp.where(at == length - 1, cond, sum_high)
     state = (
-        jnp.where(at == 0, 0.0, -before),
+        jnp.where(at == 0, 0.0, -sum_low),
         1.0 / (CZ * CZ) + left_sum + right_sum,
-        jnp.where(at == length - 1, 0.0, -after),
+        jnp.where(at == length - 1, 0.0, -sum_high),
     )
     per = stages // 2
     for stage in range(0, per):
@@ -482,8 +496,19 @@
         state = factor(state, stage)
     fac[2 * stages] = (2.0 / (CZ * CZ)) / state[1]
     finish(4, 0, None)
-    u = own_update(widen(p, 4, False))
-    rhs = pool(jnp.where(red, diag[...] * (u - p), 0.0)) * flag
+    after[...] = widen(p, 4, False)
+    residual = jnp.stack(
+        [
+            jnp.where(
+                reds[i % 2][:Y, :Z],
+                diag[i - 1] * (own_plane(after, i) - after[i, :Y, :Z]),
+                0.0,
+            )
+            for i in range(1, X + 1)
+        ],
+        axis=0,
+    )
+    rhs = pool(residual) * flag
     gather_start(rhs_all, rhs_send, 1, rhs)
     values = gather_wait(rhs_all, rhs_send, 1)
     for stage in range(stages):
@@ -553,6 +578,8 @@
             V((CHANNELS, 2, 2, Y, 128), f32),
             V((CHANNELS, 2, 2, 8, 128), f32),
             V((6, X + 2, Y + 8, Z + 128), f32),
+            V((X + 2, Y + 8, Z + 128), f32),
+            V((X + 2, Y + 8, Z + 128), f32),
             V((X, Y, Z), f32),
             V((X + 2, Y + 8, Z + 128), f32),
             V((2, X // 2 * Y, 128), f32),

time: 30.4 us -> 30.3 us (level)
  no operation moved by 1% of the time
where the time goes in v3:
time: 30.3 us; the launch traced here: 30.1 us
  Pallas kernels  28.6 us (94%)
  local copies, waits for them, and re-layouts  1.57 us (5%)
    pallas_call x1, Pallas kernels, shards(): pl.pallas_call(functools.partial(kernel, sizes), out_shape=jax.ShapeDtype...  28.6 us
    unnamed x1, local copies, waits for them, and re-layouts  1.57 us

profile of v3, /device:TPU:1, one launch (start us, length us, event | category | flops | bytes accessed | tf_op | source)
XLA Modules:
  0.0 30.1 jit_solution(9567212459931557608)
XLA Ops:
  0.0 28.6 %cycle.1 = f32[8,16,256]{2,1,0:T(8,128)} custom-call(f32[8,16,256]{2,1,0:T(8,128)} %src_hbm.1, f32[8,16,256]{2,1,0:T(8,128)} %con_hbm.1, s32[8,16,256]{2,1,0:T(8,128)} %msk_hbm.1, s32[1,1,2,16]{3,2,1,0:T(2,128)} %ids_hbm.1), custom_call_target="tpu_custom_call" | custom-call | tf_op jit(solution)/shard_map/cycle/pallas_call | solution.py:561
  28.6 1.6 %copy.6 = f32[8,16,256]{2,1,0:T(8,128)} copy(f32[8,16,256]{2,1,0:T(8,128)} %cycle.1) | data formatting | bytes 262144

commit v4 on v3

--- a/solution.py
+++ b/solution.py
@@ -246,12 +246,15 @@
                 face_copy(ch, d, side, parity).wait_send()
 
         if edge_parity is not None:
-            for e, a, b in edges:
-
-                @pl.when(has_edge(e, a, b))
-                def _():
-                    edge_copy(ch, e, a, b, edge_parity, True).wait_recv()
-                    edge_copy(ch, e, a, b, edge_parity).wait_send()
+            finish_edges(ch, edge_parity)
+
+    def finish_edges(ch, edge_parity):
+        for e, a, b in edges:
+
+            @pl.when(has_edge(e, a, b))
+            def _():
+                edge_copy(ch, e, a, b, edge_parity, True).wait_recv()
+                edge_copy(ch, e, a, b, edge_parity).wait_send()
 
     def columns(packed, xs):
         return jnp.stack(
@@ -260,6 +263,27 @@
 
     near_y = sub_y < 4
     near_z = lane_z < 64
+
+    def edge_tiles(ch):
+        yz = []
+        for side in range(2):
+            rows8 = jnp.where(near_y[0, :, :128], hyz[ch, 1, side], hyz[ch, 0, side])
+            yz.append(columns(rows8, range(X)))
+        sides = []
+        for side in range(2):
+            xy = jnp.where(
+                near_y[0],
+                jnp.broadcast_to(hxy[ch, side, 1], (8, Z)),
+                jnp.broadcast_to(hxy[ch, side, 0], (8, Z)),
+            )
+            at = 0 if side else X - 1
+            xz = jnp.where(
+                near_z[0],
+                columns(hxz[ch, side, 1], (at,))[0],
+                columns(hxz[ch, side, 0], (at,))[0],
+            )
+            sides.append((xy, xz))
+        return jnp.where(near_z[:, :8], yz[1], yz[0]), sides
 
     def widen(p, ch, with_edges, second=None):
         y_plus = jnp.broadcast_to(hy[ch, 1], (X, 8, Z))
@@ -285,11 +309,7 @@
                 jnp.where(lane_z == 127, z_minus, z_minus2),
             )
         if with_edges:
-            yz = []
-            for side in range(2):
-                rows8 = jnp.where(near_y[0, :, :128], hyz[ch, 1, side], hyz[ch, 0, side])
-                yz.append(columns(rows8, range(X)))
-            yztile = jnp.where(near_z[:, :8], yz[1], yz[0])
+            yztile, sides = edge_tiles(ch)
         else:
             yztile = jnp.zeros((X, 8, 128), jnp.float32)
         top = jnp.concatenate([p, ztile], axis=2)
@@ -297,17 +317,7 @@
         planes = []
         for side in range(2):
             if with_edges:
-                xy = jnp.where(
-                    near_y[0],
-                    jnp.broadcast_to(hxy[ch, side, 1], (8, Z)),
-                    jnp.broadcast_to(hxy[ch, side, 0], (8, Z)),
-                )
-                at = 0 if side else X - 1
-                xz = jnp.where(
-                    near_z[0],
-                    columns(hxz[ch, side, 1], (at,))[0],
-                    columns(hxz[ch, side, 0], (at,))[0],
-                )
+                xy, xz = sides[side]
             else:
                 xy = jnp.zeros((8, Z), jnp.float32)
                 xz = jnp.zeros((Y, 128), jnp.float32)
@@ -331,19 +341,30 @@
             pltpu.roll(v, 1, 1),
         )
 
+    inner_y, outer_y = slice(0, Y), slice(Y, Y + 8)
+    inner_z, outer_z = slice(0, Z), slice(Z, Z + 128)
+
+    def region(field, i, ys, zs):
+        besides = (
+            field[min(i + 1, X + 1), ys, zs],
+            field[max(i - 1, 0), ys, zs],
+            pltpu.roll(field[i, :, zs], Y + 7, 0)[ys],
+            pltpu.roll(field[i, :, zs], 1, 0)[ys],
+            pltpu.roll(field[i, ys, :], Z + 127, 1)[:, zs],
+            pltpu.roll(field[i, ys, :], 1, 1)[:, zs],
+        )
+        u = srd[i, ys, zs]
+        for k, one in enumerate(besides):
+            u = u + wts[k, i, ys, zs] * one
+        return u
+
     def own_plane(field, i):
-        besides = (
-            field[min(i + 1, X + 1), :Y, :Z],
-            field[max(i - 1, 0), :Y, :Z],
-            pltpu.roll(field[i, :, :Z], Y + 7, 0)[:Y],
-            pltpu.roll(field[i, :, :Z], 1, 0)[:Y],
-            pltpu.roll(field[i, :Y, :], Z + 127, 1)[:, :Z],
-            pltpu.roll(field[i, :Y, :], 1, 1)[:, :Z],
-        )
-        u = srd[i, :Y, :Z]
-        for k, one in enumerate(besides):
-            u = u + wts[k, i, :Y, :Z] * one
-        return u
+        return region(field, i, inner_y, inner_z)
+
+    def red_region(i, ys, zs):
+        after[i, ys, zs] = jnp.where(
+            reds[i % 2][ys, zs], region(field, i, ys, zs), field[i, ys, zs]
+        )
 
     def black_update():
         return jnp.stack(
@@ -354,20 +375,22 @@
             axis=0,
         )
 
-    def sweep(p, ch):
-        field[...] = widen(p, ch, True)
-        for i in range(X + 2):
-            mask = reds[i % 2]
-            if i in (0, X + 1):
-                after[i, :Y, :Z] = jnp.where(
-                    mask[:Y, :Z], own_plane(field, i), field[i, :Y, :Z]
-                )
-            else:
-                v = field[i]
-                u = srd[i]
-                for k, one in enumerate(around(v, field[i - 1], field[i + 1])):
-                    u = u + wts[k, i] * one
-                after[i] = jnp.where(mask, u, v)
+    def sweep(p, ch, parity, edge_parity):
+        finish(ch, parity, None)
+        field[...] = widen(p, ch, False)
+        for i in range(1, X + 1):
+            red_region(i, inner_y, inner_z)
+        finish_edges(ch, edge_parity)
+        yztile, planes = edge_tiles(ch)
+        field[1 : X + 1, Y : Y + 8, Z : Z + 128] = yztile
+        for side in range(2):
+            field[side * (X + 1), Y : Y + 8, :Z] = planes[side][0]
+            field[side * (X + 1), :Y, Z : Z + 128] = planes[side][1]
+        for i in (0, X + 1):
+            red_region(i, inner_y, inner_z)
+        for i in range(1, X + 1):
+            red_region(i, outer_y, inner_z)
+            red_region(i, inner_y, outer_z)
         return black_update()
 
     def gather_copy(buf, staged, which, off):
@@ -488,8 +511,7 @@
     per = stages // 2
     for stage in range(0, per):
         state = factor(state, stage)
-    finish(3, 1, 1)
-    p = sweep(p, 3)
+    p = sweep(p, 3, 1, 1)
     stage_black(4, p)
     start(4, 0, None)
     for stage in range(per, stages):
@@ -536,12 +558,10 @@
 
     stage_black(5, p)
     start(5, 1, 0)
-    finish(5, 1, 0)
-    p = sweep(p, 5)
+    p = sweep(p, 5, 1, 0)
     stage_black(6, p)
     start(6, 0, 1)
-    finish(6, 0, 1)
-    out_ref[...] = sweep(p, 6)
+    out_ref[...] = sweep(p, 6, 0, 1)
 
     for off in range(1, n_gz):
         gather_copy(cond_all, cond_send, 0, off).wait_send()

time: 30.3 us -> 30.1 us (level)
  no operation moved by 1% of the time
where the time goes in v4:
time: 30.1 us; the launch traced here: 29.9 us
  Pallas kernels  28.3 us (94%)
  local copies, waits for them, and re-layouts  1.57 us (5%)
    pallas_call x1, Pallas kernels, shards(): pl.pallas_call(functools.partial(kernel, sizes), out_shape=jax.ShapeDtype...  28.3 us
    unnamed x1, local copies, waits for them, and re-layouts  1.57 us

profile of v4, /device:TPU:1, one launch (start us, length us, event | category | flops | bytes accessed | tf_op | source)
XLA Modules:
  0.0 29.9 jit_solution(14853105744166338359)
XLA Ops:
  0.0 28.3 %cycle.1 = f32[8,16,256]{2,1,0:T(8,128)} custom-call(f32[8,16,256]{2,1,0:T(8,128)} %src_hbm.1, f32[8,16,256]{2,1,0:T(8,128)} %con_hbm.1, s32[8,16,256]{2,1,0:T(8,128)} %msk_hbm.1, s32[1,1,2,16]{3,2,1,0:T(2,128)} %ids_hbm.1), custom_call_target="tpu_custom_call" | custom-call | tf_op jit(solution)/shard_map/cycle/pallas_call | solution.py:581
  28.3 1.6 %copy.6 = f32[8,16,256]{2,1,0:T(8,128)} copy(f32[8,16,256]{2,1,0:T(8,128)} %cycle.1) | data formatting | bytes 262144
